TPU v7x, 128 devices: a whole 4x4x4 slice. The times are simulated.
128 devices in a mesh: seq: 32 (over z_lo, y, x), fsdp: 4 (over z_hi, core).
Axes of the slice: x: 4, y: 4, z: 4 (z_hi: 2, z_lo: 2; z = z_hi * 2 + z_lo), core: 2. Of those that a mesh axis runs over, the one named last changes fastest.
Arguments:
- tokens: bfloat16 [4, 8192, 2048], P('fsdp', 'seq'), may hold values from -6 to 6
- w_in: bfloat16 [2048, 2304], P('fsdp'), may hold values from -0.125 to 0.125
- log_decay: float32 [4, 32, 8192], P('fsdp', None, 'seq'), may hold values from -2 to 0, as said below
- grad_out: bfloat16 [4, 8192, 2048], P('fsdp', 'seq'), may hold values from -6 to 6
Outputs:
- mixer_out: bfloat16 [4, 8192, 2048], P('fsdp', 'seq')
- grad_tokens: bfloat16 [4, 8192, 2048], P('fsdp', 'seq')
- grad_weights: float32 [2048, 2304], P(('seq', 'fsdp'))
Inputs may be any that keep to these rules, and one draw needn't show every extreme that they name: `log_decay`: each entry is the logarithm of a decay factor below one.
All inputs are finite; a program needn't handle non-finite values.
Results may differ from a plain program's by a relative error of at most 0.015.
Values may be sent and summed in bfloat16 or wider, within the bound.
A program may use at most 192 MiB of HBM per device.

v0:
```python
import jax
import jax.numpy as jnp
from jax import lax
from jax.sharding import PartitionSpec as P

BLOCK = 256


highest = lax.Precision.HIGHEST
epsilon = 1e-05


def entering_2(shard, axis, join, neutral, backward):
    count = lax.axis_size(axis)
    place = lax.axis_index(axis)
    ahead = count - 1 - place if backward else place
    gathered = jax.tree.map(
        lambda a, kind: lax.all_gather(a.astype(kind), axis), shard, (jnp.bfloat16, jnp.bfloat16)
    )
    state = jax.tree.map(lambda a, e: jnp.zeros_like(a) + jnp.asarray(e, a.dtype), shard, neutral)

    def one(step, state):
        source = count - 1 - step if backward else step
        return join(
            state,
            jax.tree.map(
                lambda a, own: lax.dynamic_index_in_dim(a, source, 0, False).astype(own.dtype),
                gathered,
                shard,
            ),
        )

    return lax.fori_loop(0, ahead, one, state)


def combine_states(earlier, latter):
    return (earlier[0] + latter[0], jnp.exp(latter[0])[:, None, None] * earlier[1] + latter[1])


def block_chain(log_rates, terms, backward, start_state):

    def advance(carried, packed):
        log_k, term_k = packed
        return (jnp.exp(log_k)[:, None, None] * carried + term_k, carried)

    finish, inputs = lax.scan(advance, start_state, (log_rates, terms), reverse=backward)
    return (inputs, finish)


def decay_matrix(cumulative, log_rates):
    extent = cumulative.shape[-1]
    row_idx = lax.broadcasted_iota(jnp.int32, (extent, extent), 0)
    col_idx = lax.broadcasted_iota(jnp.int32, (extent, extent), 1)
    later_gap = cumulative[:, :, None] - cumulative[:, None, :]
    exclusive = cumulative - log_rates
    earlier_gap = exclusive[:, None, :] - exclusive[:, :, None]
    exponent = jnp.where(
        row_idx > col_idx, later_gap, jnp.where(row_idx < col_idx, earlier_gap, 0.0)
    )
    return jnp.exp(exponent) + (row_idx == col_idx).astype(jnp.float32)


def to_groups(array, axis, per_group):
    extents = array.shape
    grouped_shape = extents[:axis] + (extents[axis] // per_group, per_group) + extents[axis + 1 :]
    return jnp.moveaxis(array.reshape(grouped_shape), axis, 0)


def from_groups(array, axis):
    moved = jnp.moveaxis(array, 0, axis)
    extents = moved.shape
    return moved.reshape(
        extents[:axis] + (extents[axis] * extents[axis + 1],) + extents[axis + 2 :]
    )


def on_device(tokens, w_in, log_decay, grad_out):
    local_tokens = tokens[0]
    log_rates = log_decay[0]
    upstream_grad = grad_out[0]
    token_count = local_tokens.shape[0]
    hidden_width = local_tokens.shape[1]
    head_count = log_rates.shape[0]
    col_count = w_in.shape[1]
    inner_width = upstream_grad.shape[1]
    head_size = inner_width // head_count
    state_size = (col_count - inner_width) // 2
    block_count = token_count // BLOCK
    per_group = 8
    projected = jnp.dot(
        local_tokens,
        lax.all_gather(w_in, "fsdp", axis=0, tiled=True),
        preferred_element_type=jnp.float32,
    )
    xbc_rows = projected.astype(jnp.bfloat16)
    xbc_rows = lax.optimization_barrier(xbc_rows)
    xbc_float = xbc_rows.astype(jnp.float32)
    values = xbc_float[:, :inner_width].reshape(block_count, BLOCK, head_count, head_size)
    key_rows = xbc_float[:, inner_width : inner_width + state_size].reshape(
        block_count, BLOCK, state_size
    )
    queries = xbc_float[:, inner_width + state_size :].reshape(block_count, BLOCK, state_size)
    key_half = xbc_rows[:, inner_width : inner_width + state_size].reshape(
        block_count, BLOCK, state_size
    )
    query_half = xbc_rows[:, inner_width + state_size :].reshape(block_count, BLOCK, state_size)
    blocked = log_rates.reshape(head_count, block_count, BLOCK).transpose(1, 0, 2)
    cumulative = jnp.cumsum(blocked, axis=-1)
    totals = cumulative[:, :, -1]
    to_end = jnp.exp(totals[:, :, None] - cumulative)
    from_start = jnp.exp(cumulative - blocked)
    enter_weight = jnp.exp(cumulative)
    leave_weight = jnp.exp(totals[:, :, None] - (cumulative - blocked))
    end_terms = jnp.einsum("khq,kqhp,kqn->khpn", to_end, values, key_rows, precision=highest)
    start_terms = jnp.einsum("khq,kqhp,kqn->khpn", from_start, values, key_rows, precision=highest)
    zero_state = jnp.zeros((head_count, head_size, state_size), jnp.float32)
    none_log = jnp.zeros((head_count,), jnp.float32)
    device_log = jnp.sum(totals, axis=0)
    _, end_total = block_chain(totals, end_terms, False, zero_state)
    _, start_total = block_chain(totals, start_terms, True, zero_state)
    entering = entering_2(
        (device_log, end_total), "seq", combine_states, (none_log, zero_state), False
    )[1]
    arriving = entering_2(
        (device_log, start_total), "seq", combine_states, (none_log, zero_state), True
    )[1]
    fwd_in, _ = block_chain(totals, end_terms, False, entering)
    rev_next, _ = block_chain(totals, start_terms, True, arriving)

    def block_forward(packed):
        (
            block_vals,
            block_khalf,
            block_qhalf,
            block_queries,
            block_cumul,
            block_logs,
            block_enter,
            block_leave,
            state_in,
            state_next,
        ) = packed
        affinity = lax.dot_general(
            block_qhalf, block_khalf, (((1,), (1,)), ((), ())), preferred_element_type=jnp.float32
        )

        def group_forward(section):
            group_values, group_cumul, group_logs = section
            weighted = affinity[None] * decay_matrix(group_cumul, group_logs)
            return jnp.einsum("gij,jgp->igp", weighted, group_values, precision=highest)

        group_parts = lax.map(
            group_forward,
            (
                to_groups(block_vals, 1, per_group),
                to_groups(block_cumul, 0, per_group),
                to_groups(block_logs, 0, per_group),
            ),
        )
        inner_part = from_groups(group_parts, 1)
        carried_in = (
            jnp.einsum("qn,hpn->qhp", block_queries, state_in, precision=highest)
            * block_enter.T[:, :, None]
        )
        carried_back = (
            jnp.einsum("qn,hpn->qhp", block_queries, state_next, precision=highest)
            * block_leave.T[:, :, None]
        )
        return inner_part + carried_in + carried_back

    mixture = lax.map(
        block_forward,
        (
            values,
            key_half,
            query_half,
            queries,
            cumulative,
            blocked,
            enter_weight,
            leave_weight,
            fwd_in,
            rev_next,
        ),
    )
    row_scale = jnp.sqrt(jnp.mean(mixture * mixture, axis=-1) + epsilon)
    normed = mixture / row_scale[..., None]
    mixer_out = normed.astype(jnp.bfloat16).reshape(1, token_count, inner_width)
    upstream = upstream_grad.astype(jnp.float32).reshape(block_count, BLOCK, head_count, head_size)
    grad_mixture = (
        upstream - normed * jnp.mean(upstream * normed, axis=-1, keepdims=True)
    ) / row_scale[..., None]
    in_adjoint = jnp.einsum(
        "khq,kqhp,kqn->khpn", enter_weight, grad_mixture, queries, precision=highest
    )
    out_adjoint = jnp.einsum(
        "khq,kqhp,kqn->khpn", leave_weight, grad_mixture, queries, precision=highest
    )
    _, in_total = block_chain(totals, in_adjoint, True, zero_state)
    _, out_total = block_chain(totals, out_adjoint, False, zero_state)
    later_adjoint = entering_2(
        (device_log, in_total), "seq", combine_states, (none_log, zero_state), True
    )[1]
    earlier_adjoint = entering_2(
        (device_log, out_total), "seq", combine_states, (none_log, zero_state), False
    )[1]
    grad_ends, _ = block_chain(totals, in_adjoint, True, later_adjoint)
    grad_starts, _ = block_chain(totals, out_adjoint, False, earlier_adjoint)

    def block_backward(packed):
        (
            block_vals,
            block_keys,
            block_queries,
            block_khalf,
            block_qhalf,
            block_cumul,
            block_logs,
            block_enter,
            block_leave,
            block_end,
            block_start,
            state_in,
            state_next,
            block_grad,
            block_grad_end,
            block_grad_start,
        ) = packed
        affinity = lax.dot_general(
            block_qhalf, block_khalf, (((1,), (1,)), ((), ())), preferred_element_type=jnp.float32
        )

        def group_backward(section):
            group_values, group_cumul, group_logs, group_grad = section
            decays = decay_matrix(group_cumul, group_logs)
            weighted = affinity[None] * decays
            grad_vals = jnp.einsum("gij,igp->jgp", weighted, group_grad, precision=highest)
            grad_weighted = jnp.einsum("igp,jgp->gij", group_grad, group_values, precision=highest)
            return (grad_vals, jnp.sum(grad_weighted * decays, axis=0))

        group_vals, group_affinity = lax.map(
            group_backward,
            (
                to_groups(block_vals, 1, per_group),
                to_groups(block_cumul, 0, per_group),
                to_groups(block_logs, 0, per_group),
                to_groups(block_grad, 1, per_group),
            ),
        )
        grad_affinity = jnp.sum(group_affinity, axis=0)
        enter_cols = block_enter.T[:, :, None]
        leave_cols = block_leave.T[:, :, None]
        end_cols = block_end.T[:, :, None]
        start_cols = block_start.T[:, :, None]
        grad_queries = jnp.dot(grad_affinity, block_keys, precision=highest)
        grad_queries = grad_queries + jnp.einsum(
            "qhp,hpn->qn", block_grad * enter_cols, state_in, precision=highest
        )
        grad_queries = grad_queries + jnp.einsum(
            "qhp,hpn->qn", block_grad * leave_cols, state_next, precision=highest
        )
        grad_keys = jnp.dot(grad_affinity.T, block_queries, precision=highest)
        grad_keys = grad_keys + jnp.einsum(
            "qhp,hpn->qn", block_vals * end_cols, block_grad_end, precision=highest
        )
        grad_keys = grad_keys + jnp.einsum(
            "qhp,hpn->qn", block_vals * start_cols, block_grad_start, precision=highest
        )
        grad_values = from_groups(group_vals, 1)
        grad_values = grad_values + end_cols * jnp.einsum(
            "qn,hpn->qhp", block_keys, block_grad_end, precision=highest
        )
        grad_values = grad_values + start_cols * jnp.einsum(
            "qn,hpn->qhp", block_keys, block_grad_start, precision=highest
        )
        return (grad_values, grad_keys, grad_queries)

    grad_values, grad_keys, grad_queries = lax.map(
        block_backward,
        (
            values,
            key_rows,
            queries,
            key_half,
            query_half,
            cumulative,
            blocked,
            enter_weight,
            leave_weight,
            to_end,
            from_start,
            fwd_in,
            rev_next,
            grad_mixture,
            grad_ends,
            grad_starts,
        ),
    )
    grad_proj = jnp.concatenate(
        [
            grad_values.reshape(token_count, inner_width),
            grad_keys.reshape(token_count, state_size),
            grad_queries.reshape(token_count, state_size),
        ],
        axis=1,
    ).astype(jnp.bfloat16)
    grad_local = lax.dot_general(
        grad_proj,
        lax.all_gather(w_in, "fsdp", axis=0, tiled=True),
        (((1,), (1,)), ((), ())),
        preferred_element_type=jnp.float32,
    )
    grad_tokens = grad_local.astype(jnp.bfloat16).reshape(1, token_count, hidden_width)
    grad_weights = lax.psum_scatter(
        lax.dot_general(
            local_tokens, grad_proj, (((0,), (0,)), ((), ())), preferred_element_type=jnp.float32
        ),
        ("seq", "fsdp"),
        scatter_dimension=0,
        tiled=True,
    )
    return (mixer_out, grad_tokens, grad_weights)


def solution(mesh):
    return jax.shard_map(
        on_device,
        mesh=mesh,
        in_specs=(
            P("fsdp", "seq", None),
            P("fsdp", None),
            P("fsdp", None, "seq"),
            P("fsdp", "seq", None),
        ),
        out_specs=(P("fsdp", "seq", None), P("fsdp", "seq", None), P(("seq", "fsdp"), None)),
        check_vma=False,
    )
```

profile of v0, /device:TPU:0, one launch (start us, length us, event | category | flops | bytes accessed | tf_op | source)
XLA Modules:
  0.0 1677.7 jit_solution(10138005019356209090)
XLA Ops:
  9.2 71.4 %all-gather.11.cloned.1.call-done = bf16[2048,2304]{1,0:T(8,128)(2,1)} async-done(((bf16[512,2304]{1,0:T(8,128)(2,1)}), bf16[2048,2304]{1,0:T(8,128)(2,1)}) %all-gather.11.cloned.1.call-update) | async-done | bytes 9437200 | tf_op jit(solution)/shard_map/all_gather | solution.py:92
  80.6 6.3 convolution_convert_fusion
  103.1 81.3 %all-gather = bf16[32,32,1]{1,2,0:T(2,128)(2,1)S(1)} all-gather(bf16[1,32,1]{1,2,0:T(2,128)(2,1)S(1)} %slice.83), channel_id=2, replica_groups=mesh['seq'=32,'fsdp'=4] {'seq'}, dimensions={0}, use_global_device_ids=true | all-gather | bytes 2112 | tf_op jit(solution)/shard_map/all_gather | solution.py:18
  190.4 18.2 %while.56 = (s32[]{:T(128)}, f32[4,256,8,64]{1,3,2,0:T(8,128)}, f32[4,256,8,64]{1,3,2,0:T(8,128)S(1)}, f32[256,256]{1,0:T(8,128)}, f32[4,8,256]{2,1,0:T(8,128)S(1)}, /*index=5*/f32[4,8,256]{2,1,0:T(8,128)S(1)}, s32[]{:T(128)}) while((s32[]{:T(128)}, f32[4,256,8,64]{1,3,2,0:T(8,128)}, f32[4,256,8,64]{1,3,2,0:T(8,128)S(1)}, ...), condition=%wide.region_3.4_spmd, body=%wide.region_2.3_spmd.sunk | while | flops 406063104 | bytes 2171997 | solution.py:152
  190.4 4.5 fusion.177
  195.0 4.5 fusion.177
  199.6 4.5 fusion.177
  204.1 4.5 fusion.177
  208.6 76.7 %all-gather.15.cloned.1.call-done = bf16[1024,64,128]{2,1,0:T(8,128)(2,1)} async-done(((bf16[32,64,128]{2,1,0:T(8,128)(2,1)}), bf16[1024,64,128]{2,1,0:T(8,128)(2,1)}) %all-gather.15.cloned.1.call-update) | async-done | bytes 16777232 | tf_op jit(solution)/shard_map/all_gather | solution.py:18
  285.4 41.9 %while.58 = (s32[]{:T(128)}, f32[32,64,128]{2,1,0:T(8,128)S(1)}, s32[]{:T(128)}, bf16[32,32]{1,0:T(8,128)(2,1)S(1)}, bf16[32,32,64,128]{3,2,1,0:T(8,128)(2,1)}, ...) while((s32[]{:T(128)}, f32[32,64,128]{2,1,0:T(8,128)S(1)}, s32[]{:T(128)}, bf16[32,32]{1,0:T(8,128)(2,1)S(1)}, ...), condition=%wide.region_7.8_spmd, body=%wide.region_6.7_spmd.sunk | while | flops 786470 | bytes 2621915 | solution.py:33
  327.3 149.6 %all-gather.13.cloned.1.call-done = bf16[1024,64,128]{2,1,0:T(8,128)(2,1)} async-done(((bf16[32,64,128]{2,1,0:T(8,128)(2,1)}), bf16[1024,64,128]{2,1,0:T(8,128)(2,1)}) %all-gather.13.cloned.1.call-update) | async-done | bytes 16777232 | tf_op jit(solution)/shard_map/all_gather | solution.py:18
  488.3 3.5 fusion.87
  493.6 35.1 %while.59 = (s32[]{:T(128)}, f32[4,256,8,64]{1,3,2,0:T(8,128)}, f32[4,256,256]{2,1,0:T(8,128)}, f32[4,256,8,64]{1,3,2,0:T(8,128)}, f32[256,256]{1,0:T(8,128)}, /...) while((s32[]{:T(128)}, f32[4,256,8,64]{1,3,2,0:T(8,128)}, ...), condition=%wide.region_12.13_spmd, body=%wide.region_10.12_spmd.sunk | while | flops 812320768 | bytes 5482637 | solution.py:241
  493.7 4.0 multiply_reduce_fusion.4
  498.4 4.0 fusion.183
  502.5 4.0 multiply_reduce_fusion.4
  507.2 4.0 fusion.183
  511.3 4.0 multiply_reduce_fusion.4
  516.0 4.0 fusion.183
  520.1 4.0 multiply_reduce_fusion.4
  524.8 4.0 fusion.183
  530.1 3.7 fusion.105
  537.6 183.1 %all-gather.17.cloned.1.call-done = bf16[1024,64,128]{2,1,0:T(8,128)(2,1)} async-done(((bf16[32,64,128]{2,1,0:T(8,128)(2,1)}), bf16[1024,64,128]{2,1,0:T(8,128)(2,1)}) %all-gather.17.cloned.1.call-update) | async-done | bytes 16777232 | tf_op jit(solution)/shard_map/all_gather | solution.py:18
  720.8 42.2 %while.60 = (s32[]{:T(128)}, f32[32,64,128]{2,1,0:T(8,128)S(1)}, s32[]{:T(128)}, bf16[32,32]{1,0:T(8,128)(2,1)S(1)}, bf16[32,32,64,128]{3,2,1,0:T(8,128)(2,1)}, ...) while((s32[]{:T(128)}, f32[32,64,128]{2,1,0:T(8,128)S(1)}, s32[]{:T(128)}, ...), condition=%wide.region_14.15_spmd, body=%wide.region_13.14_spmd.sunk | while | flops 786470 | bytes 2621915 | solution.py:33
  763.0 4.3 fusion.99
  767.2 3.2 fusion.126
  770.4 140.8 %all-gather.19.cloned.1.call-done = bf16[1024,64,128]{2,1,0:T(8,128)(2,1)} async-done(((bf16[32,64,128]{2,1,0:T(8,128)(2,1)}), bf16[1024,64,128]{2,1,0:T(8,128)(2,1)}) %all-gather.19.cloned.1.call-update) | async-done | bytes 16777232 | tf_op jit(solution)/shard_map/all_gather | solution.py:18
  911.4 3.7 fusion.102
  919.1 8.7 convolution_bitcast_fusion
  927.9 18.7 %copy.74 = f32[2048,2304]{1,0:T(8,128)} copy(f32[2048,2304]{0,1:T(8,128)} %convolution_bitcast_fusion) | data formatting | bytes 37748736
  949.2 7.3 fusion.55
  956.5 714.1 %reduce-scatter.4.cloned.1.call-done = f32[16,2304]{1,0:T(8,128)} async-done(((f32[2048,2304]{1,0:T(8,128)}), f32[16,2304]{1,0:T(8,128)}) %reduce-scatter.4.cloned.1.call-update) | async-done | bytes 147472
  (261 shorter events, 134.3 us)
Async XLA Ops:
  7.2 73.4 %copy-start = (bf16[1,256,2048]{2,1,0:T(8,128)(2,1)S(1)}, bf16[1,256,2048]{2,1,0:T(8,128)(2,1)}, u32[]{:S(2)}) copy-start(bf16[1,256,2048]{2,1,0:T(8,128)(2,1)} %param.16) | copy-start | bytes 3145732
  7.2 0.8 copy-start.9
  7.2 73.4 %all-gather.11.cloned.1.call-start = ((), (), s32[]{:S(2)}) async-start(), calls=%async_computation.1 | async-start | bytes 11796480 | tf_op jit(solution)/shard_map/all_gather | solution.py:92
  7.9 277.4 %all-gather.15.cloned.1.call-start = ((), (), s32[]{:S(2)}) async-start(), calls=%async_computation.3 | async-start | bytes 17301504 | tf_op jit(solution)/shard_map/all_gather | solution.py:18
  9.1 77.8 %copy-start.11 = (f32[1,32,256]{1,2,0:T(8,128)}, f32[1,32,256]{1,2,0:T(8,128)S(1)}, u32[]{:S(2)}) copy-start(f32[1,32,256]{1,2,0:T(8,128)S(1)} %get-tuple-element.649) | copy-start | bytes 98308
  86.9 1.0 copy-start.8
  94.2 382.7 %all-gather.13.cloned.1.call-start = ((), (), s32[]{:S(2)}) async-start(), calls=%async_computation.2 | async-start | bytes 17301504 | tf_op jit(solution)/shard_map/all_gather | solution.py:18
  99.5 621.2 %all-gather.17.cloned.1.call-start = ((), (), s32[]{:S(2)}) async-start(), calls=%async_computation.4 | async-start | bytes 17301504 | tf_op jit(solution)/shard_map/all_gather | solution.py:18
  208.6 76.7 %copy-start.1 = (f32[4,256,8,64]{1,3,2,0:T(8,128)}, f32[4,256,8,64]{1,3,2,0:T(8,128)S(1)}, u32[]{:S(2)}) copy-start(f32[4,256,8,64]{1,3,2,0:T(8,128)S(1)} %get-tuple-element.1040) | copy-start | bytes 6291460
  477.5 2.0 copy-start.6
  479.5 2.3 copy-start.4
  484.1 1.4 copy-start.2
  488.3 423.0 %all-gather.19.cloned.1.call-start = ((), (), s32[]{:S(2)}) async-start(), calls=%async_computation.5 | async-start | bytes 17301504 | tf_op jit(solution)/shard_map/all_gather | solution.py:18
  491.8 1178.8 %reduce-scatter.4.cloned.1.call-start = ((), (), s32[]{:S(2)}) async-start(), calls=%async_computation.6 | async-start | bytes 19021824
  493.7 4.7 copy-start.14
  502.5 4.7 copy-start.14
  511.3 4.7 copy-start.14
  520.0 4.7 copy-start.14
  530.1 3.7 copy-start.3
  911.4 3.7 copy-start.5
  915.2 2.8 copy-start.10
  915.2 3.9 copy-start.12
  946.5 1.2 copy-start.7
  946.6 2.6 copy-start.13
Sparse Core Ops, SparseCore 0:
  9.7 70.8 all-gather.10
  94.3 190.9 all-gather.14
  287.5 189.3 all-gather.12
  488.4 232.2 all-gather.16
  722.2 189.0 all-gather.18
  946.7 723.8 reduce-scatter.3
where the time goes:
time: 1690 us; the launch traced here: 1680 us
  waiting for transfers between devices  1340 us (79%)
  matrix products  112 us (7%)
  other arithmetic  89.8 us (5%)
  blocking collectives  81.3 us (5%)
  local copies, waits for them, and re-layouts  39.6 us (2%)
    unnamed x7, waiting for transfers between devices  715 us
    all_gather x4, waiting for transfers between devices, entering_2(): lax.all_gather(a.astype(kind), axis)  550 us
    all_gather x1, blocking collectives, entering_2(): lax.all_gather(a.astype(kind), axis)  81.3 us
    add x62, other arithmetic, combine_states(): jnp.exp(latter[0])[:, None, None] * earlier[1] + latter[1]  80.9 us
    all_gather x1, waiting for transfers between devices, on_device(): lax.all_gather(w_in, 'fsdp', axis=0, tiled=True)  71.4 us
  transfers between devices with their start and end apart: 6, of which 6 were waited for; matrix products, arithmetic and copies ran while one was open for 11% of the time, Pallas kernels for 0%

commit v1 on v0

v1 whole, which is shorter than its diff:
```python
import functools
import jax
import jax.numpy as jnp
from jax import lax
from jax.experimental import pallas as pl
from jax.experimental.pallas import tpu as pltpu
from jax.sharding import PartitionSpec as P

BF = jnp.bfloat16
F32 = jnp.float32
EPS = 1e-5
H, PS, N, T, D, INNER, COLS = 32, 64, 128, 256, 2048, 2048, 2304
MESH = pl.DeviceIdType.MESH
NN = (((1,), (0,)), ((), ()))
NT = (((1,), (1,)), ((), ()))
TN = (((0,), (0,)), ((), ()))


def mm(a, b, dims):
    return lax.dot_general(a, b, dims, preferred_element_type=F32)


def place():
    s = lax.axis_index("seq")
    f = lax.axis_index("fsdp")
    return s % 4, (s // 4) % 4, s // 16, f // 2, f % 2


def device(x, y, zl, zh, core):
    return (zl * 16 + y * 4 + x, zh * 2 + core)


def flip(dim, x, y, zl, zh):
    if dim == 0:
        x = x + 1 - 2 * (x % 2)
    elif dim == 1:
        x = 3 - x
    elif dim == 2:
        y = y + 1 - 2 * (y % 2)
    elif dim == 3:
        y = 3 - y
    elif dim == 4:
        zl = 1 - zl
    else:
        zl, zh = 1 - zl, 1 - zh
    return x, y, zl, zh


def greet(peers):
    barrier = pltpu.get_barrier_semaphore()
    for peer in peers:
        pl.semaphore_signal(barrier, inc=1, device_id=peer, device_id_type=MESH)
    pl.semaphore_wait(barrier, len(peers))


def gather_kernel(w_ref, out_ref, send, recv, local):
    x, y, zl, zh, core = place()
    f = zh * 2 + core
    far_f = (1 - zh) * 2 + core
    sib = device(x, y, zl, zh, 1 - core)
    far = device(*flip(5, x, y, zl, zh), core)
    greet([sib, far])
    parts = 4
    rows = 512 // parts
    own = pltpu.make_async_copy(w_ref, out_ref.at[pl.ds(pl.multiple_of(f * 512, 512), 512)], local)
    own.start()
    started = []
    over = []
    for i in range(parts):
        here = pl.ds(i * rows, rows)
        there = pl.ds(pl.multiple_of(f * 512 + i * rows, rows), rows)
        c = pltpu.make_async_remote_copy(
            w_ref.at[here], out_ref.at[there], send.at[0, i], recv.at[0, i], far, MESH
        )
        c.start()
        over.append(c)
    for i in range(parts):
        here = pl.ds(i * rows, rows)
        there = pl.ds(pl.multiple_of(f * 512 + i * rows, rows), rows)
        c = pltpu.make_async_remote_copy(
            w_ref.at[here], out_ref.at[there], send.at[1, i], recv.at[1, i], sib, MESH
        )
        c.start()
        started.append(c)
    for i in range(parts):
        there = pl.ds(pl.multiple_of(far_f * 512 + i * rows, rows), rows)
        over[i].wait_recv()
        c = pltpu.make_async_remote_copy(
            out_ref.at[there], out_ref.at[there], send.at[2, i], recv.at[2, i], sib, MESH
        )
        c.start()
        started.append(c)
    for c in started:
        c.wait()
    for c in over:
        c.wait_send()
    own.wait()


def gather_weight(w):
    return pl.pallas_call(
        gather_kernel,
        name="gather_weight",
        out_shape=jax.ShapeDtypeStruct((D, COLS), BF),
        in_specs=[pl.BlockSpec(memory_space=pltpu.VMEM)],
        out_specs=pl.BlockSpec(memory_space=pltpu.VMEM),
        scratch_shapes=[
            pltpu.SemaphoreType.DMA((3, 4)),
            pltpu.SemaphoreType.DMA((3, 4)),
            pltpu.SemaphoreType.DMA,
        ],
        compiler_params=pltpu.CompilerParams(
            collective_id=0, has_side_effects=True, vmem_limit_bytes=40 << 20
        ),
    )(w)


def mixer_kernel(
    xt_ref, gt_ref, rows_ref, cum_ref, cumt_ref, exc_ref, exct_ref, tot_ref,
    out_ref, grad_ref,
    dec, aff, y, gm, gmw, xs, gaff, dct, dbt, bmat, cmat,
    up1, in1, down1, ent, up2, in2, down2, adj, tin,
    ssem, rsem, tsem, trsem,
):
    s = lax.axis_index("seq")
    f = lax.axis_index("fsdp")
    barrier = pltpu.get_barrier_semaphore()

    def peer(o):
        return lax.rem(s + o, 32)

    @pl.loop(1, 32)
    def _(o):
        pl.semaphore_signal(barrier, inc=1, device_id=(peer(o), f), device_id_type=MESH)

    ri = lax.broadcasted_iota(jnp.int32, (T, T), 0)
    ci = lax.broadcasted_iota(jnp.int32, (T, T), 1)
    diag = ri == ci
    for h in range(H):
        a = cum_ref[h : h + 1, :] - cumt_ref[:, h : h + 1]
        b = exct_ref[:, h : h + 1] - exc_ref[h : h + 1, :]
        e = jnp.exp(jnp.minimum(a, b))
        dec[h] = jnp.where(diag, 2.0, e).astype(BF)

    bt = xt_ref[pl.ds(INNER, N), :]
    ct = xt_ref[pl.ds(INNER + N, N), :]
    bmat[...] = bt.T
    cmat[...] = ct.T

    def head(h):
        return pl.ds(pl.multiple_of(h * PS, PS), PS)

    @pl.loop(0, H)
    def _(h):
        xv = xt_ref[head(h), :].astype(F32)
        r = rows_ref[h]
        w0 = (xv * r[2:3, :]).astype(BF)
        w1 = (xv * r[3:4, :]).astype(BF)
        xs[h, pl.ds(0, PS), :] = w1
        xs[h, pl.ds(PS, PS), :] = w0
        up1[h, pl.ds(0, PS), :] = mm(w0, bmat[...], NN).astype(BF)
        up1[h, pl.ds(PS, PS), :] = mm(w1, bmat[...], NN).astype(BF)

    pl.semaphore_wait(barrier, 31)

    def tots(o):
        p = peer(o)
        return pltpu.make_async_remote_copy(
            tot_ref.at[p], tin.at[s], tsem.at[p], trsem.at[s], (p, f), MESH
        )

    def sending(k, src, dst, o):
        p = peer(o)
        return pltpu.make_async_remote_copy(
            src.at[p], dst.at[s], ssem.at[k, p], rsem.at[k, s], (p, f), MESH
        )

    def arriving(k, src, dst, o):
        p = peer(o)
        return pltpu.make_async_remote_copy(
            src.at[p], dst.at[p], ssem.at[k, p], rsem.at[k, p], (p, f), MESH
        )

    @pl.loop(1, 32)
    def _(o):
        tots(o).start()
        sending(0, up1, in1, o).start()

    tin[s] = tot_ref[s]
    in1[s] = up1[s]

    aff[...] = mm(bmat[...], ct, NN).astype(BF)

    @pl.loop(0, H)
    def _(h):
        wt = aff[...] * dec[h]
        y[h] = mm(xt_ref[head(h), :], wt, NN)

    @pl.loop(1, 32)
    def _(o):
        p = peer(o)
        pltpu.make_async_remote_copy(
            tot_ref.at[p], tin.at[p], tsem.at[p], trsem.at[p], (p, f), MESH
        ).wait_recv()
        arriving(0, up1, in1, o).wait_recv()

    def scan(src, dst):
        def one(i, state):
            fwd, rev = state
            k = 31 - i
            dst[i, pl.ds(0, PS), :] = fwd.astype(BF)
            dst[k, pl.ds(PS, PS), :] = rev.astype(BF)
            fwd = jnp.exp(tin[i][0:1, :]) * fwd + src[i, pl.ds(0, PS), :].astype(F32)
            rev = jnp.exp(tin[k][0:1, :]) * rev + src[k, pl.ds(PS, PS), :].astype(F32)
            return fwd, rev

        zero = jnp.zeros((PS, N), F32)
        lax.fori_loop(0, 32, one, (zero, zero))

    scan(in1, down1)

    @pl.loop(1, 32)
    def _(o):
        sending(1, down1, ent, o).start()

    ent[s] = down1[s]

    @pl.loop(1, 32)
    def _(o):
        arriving(1, down1, ent, o).wait_recv()

    @pl.loop(0, H)
    def _(h):
        r = rows_ref[h]
        car = mm(ent[h], xt_ref[pl.ds(INNER + N, N), :], NN)
        mix = y[h] + r[0:1, :] * car[:PS] + r[1:2, :] * car[PS:]
        ms = jnp.sum(mix * mix, axis=0, keepdims=True) * (1.0 / PS)
        inv = 1.0 / jnp.sqrt(ms + EPS)
        z = mix * inv
        out_ref[head(h), :] = z.astype(BF)
        gv = gt_ref[head(h), :].astype(F32)
        m = jnp.sum(gv * z, axis=0, keepdims=True) * (1.0 / PS)
        gr = (gv - z * m) * inv
        gm[h] = gr.astype(BF)
        g0 = (gr * r[0:1, :]).astype(BF)
        g1 = (gr * r[1:2, :]).astype(BF)
        gmw[h, pl.ds(0, PS), :] = g0
        gmw[h, pl.ds(PS, PS), :] = g1
        up2[h, pl.ds(0, PS), :] = mm(g1, cmat[...], NN).astype(BF)
        up2[h, pl.ds(PS, PS), :] = mm(g0, cmat[...], NN).astype(BF)

    @pl.loop(1, 32)
    def _(o):
        sending(2, up2, in2, o).start()

    in2[s] = up2[s]

    gaff[...] = jnp.zeros_like(gaff)
    dct[...] = jnp.zeros_like(dct)
    dbt[...] = jnp.zeros_like(dbt)

    @pl.loop(0, H)
    def _(h):
        d = dec[h]
        wt = aff[...] * d
        g = gm[h]
        y[h] = mm(g, wt, NT)
        gw = mm(xt_ref[head(h), :], g, TN)
        gaff[...] += gw * d.astype(F32)
        dct[...] += mm(ent[h], gmw[h], TN)

    @pl.loop(1, 32)
    def _(o):
        arriving(2, up2, in2, o).wait_recv()

    scan(in2, down2)

    @pl.loop(1, 32)
    def _(o):
        sending(3, down2, adj, o).start()

    adj[s] = down2[s]
    ga = gaff[...].astype(BF)
    dct[...] += mm(xt_ref[pl.ds(INNER, N), :], ga, NN)
    dbt[...] += mm(xt_ref[pl.ds(INNER + N, N), :], ga, NT)

    @pl.loop(1, 32)
    def _(o):
        arriving(3, down2, adj, o).wait_recv()

    @pl.loop(0, H)
    def _(h):
        r = rows_ref[h]
        car = mm(adj[h], xt_ref[pl.ds(INNER, N), :], NN)
        gx = y[h] + r[3:4, :] * car[:PS] + r[2:3, :] * car[PS:]
        grad_ref[head(h), :] = gx.astype(BF)
        dbt[...] += mm(adj[h], xs[h], TN)

    grad_ref[pl.ds(INNER, N), :] = dbt[...].astype(BF)
    grad_ref[pl.ds(INNER + N, N), :] = dct[...].astype(BF)

    @pl.loop(1, 32)
    def _(o):
        tots(o).wait_send()
        sending(0, up1, in1, o).wait_send()
        sending(1, down1, ent, o).wait_send()
        sending(2, up2, in2, o).wait_send()
        sending(3, down2, adj, o).wait_send()


def mixer(xbct, gt, log):
    cum = jnp.cumsum(log, axis=1)
    exc = cum - log
    tot = cum[:, -1:]
    rows = jnp.stack(
        [jnp.exp(cum), jnp.exp(tot - exc), jnp.exp(tot - cum), jnp.exp(exc)] + [exc] * 4, axis=1
    )
    totb = jnp.broadcast_to(tot[:, :, None], (H, 8, 128))
    v = pl.BlockSpec(memory_space=pltpu.VMEM)
    st = pltpu.VMEM((H, 2 * PS, N), BF)
    return pl.pallas_call(
        mixer_kernel,
        name="mixer",
        out_shape=(
            jax.ShapeDtypeStruct((INNER, T), BF),
            jax.ShapeDtypeStruct((COLS, T), BF),
        ),
        in_specs=[v] * 8,
        out_specs=(v, v),
        scratch_shapes=[
            pltpu.VMEM((H, T, T), BF),
            pltpu.VMEM((T, T), BF),
            pltpu.VMEM((H, PS, T), F32),
            pltpu.VMEM((H, PS, T), BF),
            pltpu.VMEM((H, 2 * PS, T), BF),
            pltpu.VMEM((H, 2 * PS, T), BF),
            pltpu.VMEM((T, T), F32),
            pltpu.VMEM((N, T), F32),
            pltpu.VMEM((N, T), F32),
            pltpu.VMEM((T, N), BF),
            pltpu.VMEM((T, N), BF),
            st, st, st, st, st, st, st, st,
            pltpu.VMEM((H, 8, 128), F32),
            pltpu.SemaphoreType.DMA((4, 32)),
            pltpu.SemaphoreType.DMA((4, 32)),
            pltpu.SemaphoreType.DMA((32,)),
            pltpu.SemaphoreType.DMA((32,)),
        ],
        compiler_params=pltpu.CompilerParams(
            collective_id=1, has_side_effects=True, vmem_limit_bytes=56 << 20
        ),
    )(xbct, gt, rows, cum, cum.T, exc, exc.T, totb)


CW = COLS // 6
OFF = [0, 32, 48, 56, 60, 62]


def order(color):
    dims = [(color + k) % 6 for k in range(6)]
    found = []
    for i in range(64):
        r = 0
        for k in range(6):
            if (i >> (5 - k)) & 1:
                r |= 1 << dims[k]
        found.append(r)
    return found


def wgrad_kernel(tok_ref, g_ref, out_ref, ta, tb, ts, gs, acc, sb, rb, ssem, rsem, xs, xr):
    x, y, zl, zh, core = place()
    sib = device(x, y, zl, zh, 1 - core)
    peers = [device(*flip(d, x, y, zl, zh), core) for d in range(6)]
    greet(peers + [sib])
    c0 = pltpu.make_async_remote_copy(g_ref, gs, xs.at[0], xr.at[0], sib, MESH)
    c1 = pltpu.make_async_remote_copy(tok_ref.at[1 - core], ts, xs.at[1], xr.at[1], sib, MESH)
    c1.start()
    c0.start()

    def block(r):
        p = (x, y, zl, zh)
        for d in range(6):
            if (r >> d) & 1:
                p = flip(d, *p)
        return p[2] * 32 + p[1] * 8 + p[0] * 2 + p[3]

    for r in range(64):
        ta[r] = tok_ref[core, block(r)]
    c1.wait_recv()
    for r in range(64):
        tb[r] = ts[block(r)]
    c0.wait_recv()

    def product(c, half):
        ids = order(c)[32 * half : 32 * half + 32]
        la = jnp.concatenate([ta[r] for r in ids], axis=0)
        lb = jnp.concatenate([tb[r] for r in ids], axis=0)
        cols = pl.ds(c * CW, CW)
        return (mm(la, g_ref[:, cols], NN) + mm(lb, gs[:, cols], NN)).reshape(32, 16, CW)

    def copy(c, k):
        n = 32 >> k
        part = pl.ds(OFF[k], n)
        return pltpu.make_async_remote_copy(
            sb.at[c, part], rb.at[c, part], ssem.at[c, k], rsem.at[c, k], peers[(c + k) % 6], MESH
        )

    for c in range(6):
        sb[c, pl.ds(0, 32)] = product(c, 1).astype(BF)
        copy(c, 0).start()
    for c in range(6):
        acc[c] = product(c, 0)
    for k in range(1, 6):
        n = 64 >> k
        m = n // 2
        for c in range(6):
            copy(c, k - 1).wait_recv()
            hi = acc[c, pl.ds(m, m)] + rb[c, pl.ds(OFF[k - 1] + m, m)].astype(F32)
            sb[c, pl.ds(OFF[k], m)] = hi.astype(BF)
            copy(c, k).start()
        for c in range(6):
            acc[c, pl.ds(0, m)] += rb[c, pl.ds(OFF[k - 1], m)].astype(F32)
    for c in range(6):
        copy(c, 5).wait_recv()
        out_ref[:, pl.ds(c * CW, CW)] = acc[c, 0] + rb[c, OFF[5]].astype(F32)
    for c in range(6):
        for k in range(6):
            copy(c, k).wait_send()
    c0.wait_send()
    c1.wait_send()


def weight_gradient(tokt, g):
    v = pl.BlockSpec(memory_space=pltpu.VMEM)
    return pl.pallas_call(
        wgrad_kernel,
        name="weight_gradient",
        out_shape=jax.ShapeDtypeStruct((16, COLS), F32),
        in_specs=[v, v],
        out_specs=v,
        scratch_shapes=[
            pltpu.VMEM((64, 16, T), BF),
            pltpu.VMEM((64, 16, T), BF),
            pltpu.VMEM((64, 16, T), BF),
            pltpu.VMEM((T, COLS), BF),
            pltpu.VMEM((6, 32, 16, CW), F32),
            pltpu.VMEM((6, 63, 16, CW), BF),
            pltpu.VMEM((6, 63, 16, CW), BF),
            pltpu.SemaphoreType.DMA((6, 6)),
            pltpu.SemaphoreType.DMA((6, 6)),
            pltpu.SemaphoreType.DMA((2,)),
            pltpu.SemaphoreType.DMA((2,)),
        ],
        compiler_params=pltpu.CompilerParams(
            collective_id=2, has_side_effects=True, vmem_limit_bytes=48 << 20
        ),
    )(tokt, g)


def on_device(tokens, w_in, log_decay, grad_out):
    tok = tokens[0]
    w = gather_weight(w_in)
    xbct = mm(w, tok, (((0,), (1,)), ((), ()))).astype(BF)
    tokt = tok.T.reshape(64, 2, 16, T).transpose(1, 0, 2, 3)
    outt, gradt = mixer(xbct, grad_out[0].T, log_decay[0])
    g = gradt.T
    grad_w = weight_gradient(tokt, g)
    grad_tokens = mm(g, w, NT).astype(BF)
    return outt.T[None], grad_tokens[None], grad_w


def solution(mesh):
    return jax.shard_map(
        on_device,
        mesh=mesh,
        in_specs=(
            P("fsdp", "seq", None),
            P("fsdp", None),
            P("fsdp", None, "seq"),
            P("fsdp", "seq", None),
        ),
        out_specs=(P("fsdp", "seq", None), P("fsdp", "seq", None), P(("seq", "fsdp"), None)),
        check_vma=False,
    )
```

time: 1690 us -> 225 us (0.13)
  waiting for transfers between devices: 1340 us -> 0 us
  Pallas kernels: 0 us -> 197 us
  matrix products: 112 us -> 11.4 us
  other arithmetic: 89.8 us -> 0.96 us
  blocking collectives: 81.3 us -> 0 us
  local copies, waits for them, and re-layouts: 39.6 us -> 15.3 us
    unnamed x7 -> x0, waiting for transfers between devices: 715 us -> none
    all_gather x5 -> x0, waiting for transfers between devices: 622 us -> none  [the longest x4 550 us: entering_2(): lax.all_gather(a.astype(kind), axis)]
    pallas_call x0 -> x3, Pallas kernels: none -> 197 us  [the longest x1 97.5 us: mixer(): pl.pallas_call(mixer_kernel, name='mixer', out_shape=(jax.ShapeDtypeStruc...]
    dot_general x30 -> x2, matrix products: 112 us -> 11.4 us  [mm(): return lax.dot_general(a, b, dims, preferred_element_type=F32)]
    all_gather x1 -> x0, blocking collectives: 81.3 us -> none  [entering_2(): lax.all_gather(a.astype(kind), axis)]
    add x62 -> x0, other arithmetic: 80.9 us -> none  [combine_states(): jnp.exp(latter[0])[:, None, None] * earlier[1] + latter[1]]
  transfers between devices with their start and end apart: 6 -> 0, of which waited for: 6 -> 0; matrix products, arithmetic and copies ran while one was open for 11% -> 0% of each run, Pallas kernels for 0% -> 0%
where the time goes in v1:
time: 225 us
  Pallas kernels  197 us (88%)
  local copies, waits for them, and re-layouts  15.3 us (7%)
  matrix products  11.4 us (5%)
    pallas_call x1, Pallas kernels, mixer(): pl.pallas_call(mixer_kernel, name='mixer', out_shape=(jax.ShapeDtypeStruc...  97.5 us
    pallas_call x1, Pallas kernels, gather_weight(): pl.pallas_call(gather_kernel, name='gather_weight', out_shape=jax.ShapeDt...  58.1 us
    pallas_call x1, Pallas kernels, weight_gradient(): pl.pallas_call(wgrad_kernel, name='weight_gradient', out_shape=jax.ShapeD...  41.1 us
    dot_general x2, matrix products, mm(): return lax.dot_general(a, b, dims, preferred_element_type=F32)  11.4 us
    unnamed x21, local copies, waits for them, and re-layouts  10.8 us

profile of v1, /device:TPU:0, one launch (start us, length us, event | category | flops | bytes accessed | tf_op | source)
XLA Modules:
  0.0 225.1 jit_solution(3337052005074366782)
XLA Ops:
  0.6 0.0 copy-start.1
  0.6 1.7 copy-done.1
  2.3 58.1 %gather_weight.1 = bf16[2048,2304]{1,0:T(8,128)(2,1)S(1)} custom-call(bf16[512,2304]{1,0:T(8,128)(2,1)S(1)} %copy-done.1), custom_call_target="tpu_custom_call" | custom-call | tf_op jit(solution)/shard_map/gather_weight/pallas_call | solution.py:101
  60.4 0.0 copy-start
  60.4 3.6 %copy-done = bf16[2048,2304]{1,0:T(8,128)(2,1)} copy-done((bf16[2048,2304]{1,0:T(8,128)(2,1)}, bf16[2048,2304]{1,0:T(8,128)(2,1)S(1)}, u32[]{:S(2)}) %copy-start) | copy-done | bytes 9437208
  64.0 0.0 copy-done.6
  64.0 3.7 %convolution_convert_fusion.xt_ref = bf16[2304,256]{1,0:T(8,128)(2,1)} fusion(bf16[2048,2304]{1,0:T(8,128)(2,1)S(1)} %gather_weight.1, bf16[1,256,2048]{2,1,0:T(8,128)(2,1)S(1)} %copy-done.6), kind=kOutput, calls=%fused_computation | convolution fusion | flops 2416508928 | bytes 11665408 | tf_op jit(solution)/shard_map/dot_general | solution.py:20
  67.7 0.0 copy-done.5
  67.7 1.3 copy.17
  69.0 0.0 copy-done.7
  69.1 0.6 reduce-window.6
  69.7 0.2 slice_reduce_fusion
  69.9 0.1 broadcast_add_fusion
  70.0 0.1 copy.20
  70.1 0.0 copy-start.2
  70.1 0.1 fusion.2
  70.2 0.1 subtract_exponential_fusion.1
  70.4 1.1 stack.2.rows_ref
  71.4 0.7 copy.22.cum_ref
  72.1 0.1 copy.21
  72.2 0.0 copy-start.3
  72.2 0.7 copy.23.exc_ref
  72.9 0.8 broadcast_in_dim.12.tot_ref
  73.7 97.5 %mixer.1 = (bf16[2048,256]{1,0:T(8,128)(2,1)}, bf16[2304,256]{1,0:T(8,128)(2,1)}) custom-call(bf16[2304,256]{1,0:T(8,128)(2,1)} %convolution_convert_fusion.xt_ref, bf16[2048,256]{1,0:T(8,128)(2,1)} %bitcast.35, f32[32,8,256]{2,1,0:T(8,128)} %stack.2.rows_ref, f32[32,256]{1,0:T(8,128)} %copy.22.cum_ref, f32[256,32]{1,0:T(8,128)} %bitcast.39, ...), custom_call_target="tpu_custom_call" | custom-call | tf_op jit(solution)/shard_map/mixer/pallas_call | solution.py:321
  171.1 2.3 %copy.26 = bf16[1,256,2048]{2,1,0:T(8,128)(2,1)} copy(bf16[1,256,2048]{1,2,0:T(8,128)(2,1)} %bitcast.41) | data formatting | bytes 2097152
  173.4 7.7 %fusion = bf16[1,256,2048]{2,1,0:T(8,128)(2,1)} fusion(bf16[2304,256]{1,0:T(8,128)(2,1)} %get-tuple-element.6, bf16[2048,2304]{1,0:T(8,128)(2,1)} %copy-done), kind=kOutput, calls=%fused_computation.2 | convolution fusion | flops 2416443392 | bytes 11665408 | tf_op jit(solution)/shard_map/dot_general | solution.py:20
  181.1 0.5 copy.16
  181.6 0.1 copy.28
  181.7 0.7 copy-done.4
  182.4 0.9 copy.25
  183.3 41.1 %weight_gradient.1 = f32[16,2304]{1,0:T(8,128)S(1)} custom-call(bf16[2,64,16,256]{3,2,1,0:T(8,128)(2,1)S(1)} %bitcast.34, bf16[256,2304]{1,0:T(8,128)(2,1)S(1)} %bitcast.33), custom_call_target="tpu_custom_call" | custom-call | tf_op jit(solution)/shard_map/weight_gradient/pallas_call | solution.py:436
  224.4 0.7 copy.30
  (13 shorter events, 0.1 us)
Async XLA Ops:
  0.6 1.7 copy-start.1
  2.3 61.7 %copy-start.6 = (bf16[1,256,2048]{2,1,0:T(8,128)(2,1)S(1)}, bf16[1,256,2048]{2,1,0:T(8,128)(2,1)}, u32[]{:S(2)}) copy-start(bf16[1,256,2048]{2,1,0:T(8,128)(2,1)} %param.4) | copy-start | bytes 3145732
  60.4 3.6 %copy-start = (bf16[2048,2304]{1,0:T(8,128)(2,1)}, bf16[2048,2304]{1,0:T(8,128)(2,1)S(1)}, u32[]{:S(2)}) copy-start(bf16[2048,2304]{1,0:T(8,128)(2,1)S(1)} %gather_weight.1) | copy-start | bytes 28311556
  64.0 3.7 %copy-start.5 = (bf16[1,256,2048]{2,1,0:T(8,128)(2,1)S(1)}, bf16[1,256,2048]{2,1,0:T(8,128)(2,1)}, u32[]{:S(2)}) copy-start(bf16[1,256,2048]{2,1,0:T(8,128)(2,1)} %param.7) | copy-start | bytes 3145732
  64.0 5.0 %copy-start.7 = (f32[1,32,256]{2,1,0:T(8,128)S(1)}, f32[1,32,256]{2,1,0:T(8,128)}, u32[]{:S(2)}) copy-start(f32[1,32,256]{2,1,0:T(8,128)} %param.6) | copy-start | bytes 98308
  70.1 3.6 %copy-start.2 = (f32[32,2,128]{0,2,1:T(8,128)}, f32[32,2,128]{0,2,1:T(8,128)S(1)}, u32[]{:S(2)}) copy-start(f32[32,2,128]{0,2,1:T(8,128)S(1)} %copy.20) | copy-start | bytes 98308
  72.2 1.4 copy-start.3
  181.1 1.3 copy-start.4

commit v2 on v1

v2 whole, which is shorter than its diff:
```python
import functools
import jax
import jax.numpy as jnp
from jax import lax
from jax.experimental import pallas as pl
from jax.experimental.pallas import tpu as pltpu
from jax.sharding import PartitionSpec as P

BF = jnp.bfloat16
F32 = jnp.float32
EPS = 1e-5
H, PS, N, T, D, INNER, COLS = 32, 64, 128, 256, 2048, 2048, 2304
MESH = pl.DeviceIdType.MESH
NN = (((1,), (0,)), ((), ()))
NT = (((1,), (1,)), ((), ()))
TN = (((0,), (0,)), ((), ()))
CW = COLS // 6
OFF = [0, 32, 48, 56, 60, 62]
SUB = 4
ROWS = 128 // SUB


def mm(a, b, dims):
    return lax.dot_general(a, b, dims, preferred_element_type=F32)


def place():
    s = lax.axis_index("seq")
    f = lax.axis_index("fsdp")
    return s % 4, (s // 4) % 4, s // 16, f // 2, f % 2


def device(x, y, zl, zh, core):
    return (zl * 16 + y * 4 + x, zh * 2 + core)


def flip(dim, x, y, zl, zh):
    if dim == 0:
        x = x + 1 - 2 * (x % 2)
    elif dim == 1:
        x = 3 - x
    elif dim == 2:
        y = y + 1 - 2 * (y % 2)
    elif dim == 3:
        y = 3 - y
    elif dim == 4:
        zl = 1 - zl
    else:
        zl, zh = 1 - zl, 1 - zh
    return x, y, zl, zh


def order(color):
    dims = [(color + k) % 6 for k in range(6)]
    found = []
    for i in range(64):
        r = 0
        for k in range(6):
            if (i >> (5 - k)) & 1:
                r |= 1 << dims[k]
        found.append(r)
    return found


def remote(src, dst, ssem, rsem, to):
    return pltpu.make_async_remote_copy(src, dst, ssem, rsem, to, MESH)


def kernel(
    tok_hbm, w_hbm, log_ref, go_hbm,
    out_hbm, gt_hbm, gw_ref,
    wf, tok, tokt, ts, ta, tb, go, gtr, acc, xt, rows, tot, tin,
    dec, aff, y, gm, gmw, xs, gaff, dct, dbt, bmat, cmat,
    up1, in1, down1, ent, up2, in2, down2, adj,
    outt, outn, grad, g, gs, part, sb, rb,
    lsem, far_s, far_r, nb_s, nb_r, sf_s, sf_r, sib_s, sib_r,
    ssem, rsem, tsem, trsem, wsem, wrsem,
):
    s = lax.axis_index("seq")
    f = lax.axis_index("fsdp")
    x, y_, zl, zh, core = place()
    here = (x, y_, zl, zh)
    sib = device(*here, 1 - core)
    far = device(*flip(5, *here), core)
    peers = [device(*flip(d, *here), core) for d in range(6)]
    barrier = pltpu.get_barrier_semaphore()

    def peer(o, sign=1):
        px = lax.rem(x + 4 + sign * (o % 4), 4)
        py = lax.rem(y_ + 4 + sign * ((o // 4) % 4), 4)
        pz = lax.rem(zl + o // 16, 2)
        return pz * 16 + py * 4 + px

    @pl.loop(1, 32)
    def _(o):
        pl.semaphore_signal(barrier, inc=1, device_id=(peer(o), f), device_id_type=MESH)

    for q in (sib, far):
        pl.semaphore_signal(barrier, inc=1, device_id=q, device_id_type=MESH)

    def whole(i):
        return pl.ds(pl.multiple_of(i * 512, 512), 512)

    tok_in = pltpu.make_async_copy(tok_hbm, tok, lsem.at[0])
    go_in = pltpu.make_async_copy(go_hbm, go, lsem.at[1])
    own_in = pltpu.make_async_copy(w_hbm, wf.at[whole(f)], lsem.at[2])
    tok_in.start()
    own_in.start()
    go_in.start()

    ri = lax.broadcasted_iota(jnp.int32, (T, T), 0)
    ci = lax.broadcasted_iota(jnp.int32, (T, T), 1)
    log = log_ref[...]
    cum = lax.dot_general(
        log, (ri <= ci).astype(F32), NN, precision=lax.Precision.HIGHEST, preferred_element_type=F32
    )
    exc = cum - log
    last = cum[:, T - 1 : T]
    cumt = cum.T
    exct = exc.T
    fac = (jnp.exp(cum), jnp.exp(last - exc), jnp.exp(last - cum), jnp.exp(exc))
    lastb = jnp.broadcast_to(last, (H, N))
    for h in range(H):
        for k in range(4):
            rows[h, k : k + 1, :] = fac[k][h : h + 1, :]
        tot[h] = jnp.broadcast_to(lastb[h : h + 1, :], (8, N))

    pl.semaphore_wait(barrier, 33)

    far_f = (1 - zh) * 2 + core
    sibfar_f = (1 - zh) * 2 + 1 - core
    q0, q1 = (x + zl) % 2, (y_ + zl) % 2
    colour = q0 + 2 * q1
    others = [(1 - q0) + 2 * q1, q0 + 2 * (1 - q1), (1 - q0) + 2 * (1 - q1)]
    ndims = [0, 2, 4]

    def piece(shard, quarter, i):
        return pl.ds(pl.multiple_of(shard * 512 + quarter * 128 + i * ROWS, ROWS), ROWS)

    def far_copy(i):
        mine = pl.ds(pl.multiple_of(others[2] * 128 + i * ROWS, ROWS), ROWS)
        return remote(
            w_hbm.at[mine], wf.at[piece(f, others[2], i)], far_s.at[i], far_r.at[i], far
        )

    def near_copy(d, i):
        p = piece(far_f, colour, i)
        return remote(wf.at[p], wf.at[p], nb_s.at[d, i], nb_r.at[d, i], peers[ndims[d]])

    def pass_copy(j, i):
        p = piece(far_f, colour if j == 0 else others[j - 1], i)
        return remote(wf.at[p], wf.at[p], sf_s.at[j, i], sf_r.at[j, i], sib)

    own_out = remote(w_hbm, wf.at[whole(f)], sib_s.at[0], sib_r.at[0], sib)
    for i in range(SUB):
        far_copy(i).start()
    own_out.start()

    @pl.loop(1, 32)
    def _(o):
        p = peer(o)
        remote(tot.at[p], tin.at[s], tsem.at[p], trsem.at[s], (p, f)).start()

    tin[s] = tot[s]

    diag = ri == ci

    def decays(h):
        a = cum[h : h + 1, :] - cumt[:, h : h + 1]
        b = exct[:, h : h + 1] - exc[h : h + 1, :]
        e = jnp.exp(jnp.minimum(a, b))
        dec[h] = jnp.where(diag, 2.0, e).astype(BF)

    tok_in.wait()
    for c in range(16):
        tt = tok[:, 128 * c : 128 * c + 128].T
        for k in range(8):
            b = 8 * c + k
            tokt[b % 2, b // 2] = tt[16 * k : 16 * k + 16, :]
    tok_out = remote(tokt.at[1 - core], ts, sib_s.at[1], sib_r.at[1], sib)
    tok_out.start()

    for i in range(SUB):
        far_copy(i).wait_recv()
        for d in range(3):
            near_copy(d, i).start()
        pass_copy(0, i).start()
        for h in range(8 * i, 8 * i + 8):
            decays(h)

    def project(shard, first):
        k = pl.ds(pl.multiple_of(shard * 512, 512), 512)
        for c in range(3):
            cols = pl.ds(768 * c, 768)
            v = mm(tok[:, k], wf[k, cols], NN)
            if first:
                acc[:, cols] = v
            else:
                acc[:, cols] += v

    own_in.wait()
    project(f, True)
    for i in range(SUB):
        for d in range(3):
            remote(
                wf.at[piece(far_f, others[d], i)], wf.at[piece(far_f, others[d], i)],
                nb_s.at[d, i], nb_r.at[d, i], peers[ndims[d]],
            ).wait_recv()
            pass_copy(1 + d, i).start()
    go_in.wait()
    for c in range(16):
        gtr[128 * c : 128 * c + 128, :] = go[:, 128 * c : 128 * c + 128].T
    own_out.wait_recv()
    project(zh * 2 + 1 - core, False)
    project(far_f, False)
    for i in range(SUB):
        for j in range(4):
            p = piece(sibfar_f, colour if j == 0 else others[j - 1], i)
            remote(wf.at[p], wf.at[p], sf_s.at[j, i], sf_r.at[j, i], sib).wait_recv()
    project(sibfar_f, False)

    bmat[...] = acc[:, INNER : INNER + N].astype(BF)
    cmat[...] = acc[:, INNER + N : COLS].astype(BF)
    for c in range(18):
        xt[128 * c : 128 * c + 128, :] = acc[:, 128 * c : 128 * c + 128].astype(BF).T

    def head(h):
        return pl.ds(pl.multiple_of(h * PS, PS), PS)

    def sending(k, src, dst, p):
        return remote(src.at[p], dst.at[s], ssem.at[k, p], rsem.at[k, s], (p, f))

    def arriving(k, src, dst, p):
        return remote(src.at[p], dst.at[p], ssem.at[k, p], rsem.at[k, p], (p, f))

    def staged(k, src, dst, sign, wait, compute):
        def ship(t):
            @pl.when(t > 0)
            def _():
                sending(k, src, dst, peer(2 * t, sign)).start()

            sending(k, src, dst, peer(2 * t + 1, sign)).start()

        @pl.loop(0, 16)
        def _(t):
            if wait is not None:

                @pl.when(t > 0)
                def _():
                    arriving(*wait, peer(2 * t, sign)).wait_recv()

                arriving(*wait, peer(2 * t + 1, sign)).wait_recv()
            compute([peer(2 * t, sign), peer(2 * t + 1, sign)])
            if dst is not None:

                @pl.when(t > 0)
                def _():
                    ship(t - 1)

        if dst is not None:
            ship(15)

    def state(hs):
        for h in hs:
            xv = xt[head(h), :].astype(F32)
            r = rows[h]
            xs[h, pl.ds(0, PS), :] = (xv * r[2:3, :]).astype(BF)
            xs[h, pl.ds(PS, PS), :] = (xv * r[3:4, :]).astype(BF)
        for h in hs:
            up1[h] = mm(xs[h], bmat[...], NN).astype(BF)

    staged(0, up1, in1, 1, None, state)
    in1[s] = up1[s]

    aff[...] = mm(bmat[...], xt[pl.ds(INNER + N, N), :], NN).astype(BF)

    @pl.loop(0, H // 2)
    def _(t):
        for h in (2 * t, 2 * t + 1):
            y[h] = mm(xt[head(h), :], aff[...] * dec[h], NN)

    @pl.loop(1, 32)
    def _(o):
        p = peer(o)
        remote(tot.at[p], tin.at[p], tsem.at[p], trsem.at[p], (p, f)).wait_recv()
        arriving(0, up1, in1, p).wait_recv()

    def scan(src, dst, fwd, rev):
        def one(i, carry):
            a, b = carry
            k = 31 - i
            dst[i, pl.ds(fwd, PS), :] = a.astype(BF)
            dst[k, pl.ds(rev, PS), :] = b.astype(BF)
            a = jnp.exp(tin[i][0:1, :]) * a + src[i, pl.ds(fwd, PS), :].astype(F32)
            b = jnp.exp(tin[k][0:1, :]) * b + src[k, pl.ds(rev, PS), :].astype(F32)
            return a, b

        zero = jnp.zeros((PS, N), F32)
        lax.fori_loop(0, 32, one, (zero, zero))

    scan(in1, down1, 0, PS)

    @pl.loop(1, 32)
    def _(o):
        sending(1, down1, ent, peer(o)).start()

    ent[s] = down1[s]

    def mixture(hs):
        for h in hs:
            r = rows[h]
            car = mm(ent[h], xt[pl.ds(INNER + N, N), :], NN)
            mix = y[h] + r[0:1, :] * car[:PS] + r[1:2, :] * car[PS:]
            ms = jnp.sum(mix * mix, axis=0, keepdims=True) * (1.0 / PS)
            inv = 1.0 / jnp.sqrt(ms + EPS)
            z = mix * inv
            outt[head(h), :] = z.astype(BF)
            gv = gtr[head(h), :].astype(F32)
            m = jnp.sum(gv * z, axis=0, keepdims=True) * (1.0 / PS)
            gr = (gv - z * m) * inv
            gm[h] = gr.astype(BF)
            gmw[h, pl.ds(0, PS), :] = (gr * r[0:1, :]).astype(BF)
            gmw[h, pl.ds(PS, PS), :] = (gr * r[1:2, :]).astype(BF)
        for h in hs:
            up2[h] = mm(gmw[h], cmat[...], NN).astype(BF)

    staged(2, up2, in2, -1, (1, down1, ent), mixture)
    in2[s] = up2[s]

    gaff[...] = jnp.zeros_like(gaff)
    dct[...] = jnp.zeros_like(dct)
    dbt[...] = jnp.zeros_like(dbt)

    @pl.loop(0, H // 2)
    def _(t):
        total = None
        for h in (2 * t, 2 * t + 1):
            d = dec[h]
            gh = gm[h]
            y[h] = mm(gh, aff[...] * d, NT)
            gw = mm(xt[head(h), :], gh, TN) * d.astype(F32)
            total = gw if total is None else total + gw
        gaff[...] += total
        pair = pl.ds(2 * t, 2)
        dct[...] += mm(ent[pair].reshape(256, N), gmw[pair].reshape(256, T), TN)

    for c in range(16):
        outn[:, 128 * c : 128 * c + 128] = outt[128 * c : 128 * c + 128, :].T
    out_copy = pltpu.make_async_copy(outn, out_hbm, lsem.at[3])
    out_copy.start()

    tok_out.wait_recv()

    def block(r):
        p = here
        for d in range(6):
            if (r >> d) & 1:
                p = flip(d, *p)
        return p[2] * 32 + p[1] * 8 + p[0] * 2 + p[3]

    for r in range(64):
        b = block(r)
        ta[r] = tokt[core, b]
        tb[r] = ts[b]

    @pl.loop(1, 32)
    def _(o):
        arriving(2, up2, in2, peer(o)).wait_recv()

    scan(in2, down2, PS, 0)

    @pl.loop(1, 32)
    def _(o):
        sending(3, down2, adj, peer(o)).start()

    adj[s] = down2[s]
    ga = gaff[...].astype(BF)
    dct[...] += mm(xt[pl.ds(INNER, N), :], ga, NN)
    dbt[...] += mm(xt[pl.ds(INNER + N, N), :], ga, NT)
    g[:, INNER + N : COLS] = dct[...].astype(BF).T

    def finish(hs):
        total = None
        for h in hs:
            r = rows[h]
            car = mm(adj[h], xt[pl.ds(INNER, N), :], NN)
            gx = y[h] + r[2:3, :] * car[:PS] + r[3:4, :] * car[PS:]
            grad[head(h), :] = gx.astype(BF)
            v = mm(adj[h], xs[h], TN)
            total = v if total is None else total + v
        dbt[...] += total

    staged(3, None, None, -1, (3, down2, adj), finish)
    for c in range(16):
        g[:, 128 * c : 128 * c + 128] = grad[128 * c : 128 * c + 128, :].T
    g[:, INNER : INNER + N] = dbt[...].astype(BF).T

    g_out = remote(g, gs, sib_s.at[2], sib_r.at[2], sib)
    g_out.start()

    def tokens_part(i):
        r = pl.ds(512 * i, 512)
        tok[:, r] = mm(g[...], wf[r, :], NT).astype(BF)

    tokens_part(0)
    tokens_part(1)
    g_out.wait_recv()

    def product(c, half):
        ids = order(c)[32 * half : 32 * half + 32]
        la = jnp.concatenate([ta[r] for r in ids], axis=0)
        lb = jnp.concatenate([tb[r] for r in ids], axis=0)
        cols = pl.ds(c * CW, CW)
        return (mm(la, g[:, cols], NN) + mm(lb, gs[:, cols], NN)).reshape(32, 16, CW)

    def halve(c, k):
        p = pl.ds(OFF[k], 32 >> k)
        return remote(sb.at[c, p], rb.at[c, p], wsem.at[c, k], wrsem.at[c, k], peers[(c + k) % 6])

    for c in range(6):
        sb[c, pl.ds(0, 32)] = product(c, 1).astype(BF)
        halve(c, 0).start()
    for c in range(6):
        part[c] = product(c, 0)
    tokens_part(2)
    tokens_part(3)
    gt_copy = pltpu.make_async_copy(tok, gt_hbm, lsem.at[4])
    gt_copy.start()
    for k in range(1, 6):
        n = 64 >> k
        m = n // 2
        for c in range(6):
            halve(c, k - 1).wait_recv()
            hi = part[c, pl.ds(m, m)] + rb[c, pl.ds(OFF[k - 1] + m, m)].astype(F32)
            sb[c, pl.ds(OFF[k], m)] = hi.astype(BF)
            halve(c, k).start()
        for c in range(6):
            part[c, pl.ds(0, m)] += rb[c, pl.ds(OFF[k - 1], m)].astype(F32)
    for c in range(6):
        halve(c, 5).wait_recv()
        gw_ref[:, pl.ds(c * CW, CW)] = part[c, 0] + rb[c, OFF[5]].astype(F32)

    for i in range(SUB):
        far_copy(i).wait_send()
        for d in range(3):
            near_copy(d, i).wait_send()
        for j in range(4):
            pass_copy(j, i).wait_send()
    own_out.wait_send()
    tok_out.wait_send()
    g_out.wait_send()

    @pl.loop(1, 32)
    def _(o):
        p = peer(o)
        remote(tot.at[p], tin.at[s], tsem.at[p], trsem.at[s], (p, f)).wait_send()
        sending(0, up1, in1, p).wait_send()
        sending(1, down1, ent, p).wait_send()
        sending(2, up2, in2, p).wait_send()
        sending(3, down2, adj, p).wait_send()

    for c in range(6):
        for k in range(6):
            halve(c, k).wait_send()
    out_copy.wait()
    gt_copy.wait()


def on_device(tokens, w_in, log_decay, grad_out):
    v = pl.BlockSpec(memory_space=pltpu.VMEM)
    a = pl.BlockSpec(memory_space=pl.ANY)
    vm = pltpu.VMEM
    st = vm((H, 2 * PS, N), BF)
    dma = pltpu.SemaphoreType.DMA
    out, gt, gw = pl.pallas_call(
        kernel,
        name="mixer_step",
        out_shape=(
            jax.ShapeDtypeStruct((T, INNER), BF),
            jax.ShapeDtypeStruct((T, D), BF),
            jax.ShapeDtypeStruct((16, COLS), F32),
        ),
        in_specs=[a, a, v, a],
        out_specs=(a, a, v),
        scratch_shapes=[
            vm((D, COLS), BF),
            vm((T, D), BF),
            vm((2, 64, 16, T), BF),
            vm((64, 16, T), BF),
            vm((64, 16, T), BF),
            vm((64, 16, T), BF),
            vm((T, INNER), BF),
            vm((INNER, T), BF),
            vm((T, COLS), F32),
            vm((COLS, T), BF),
            vm((H, 8, T), F32),
            vm((H, 8, N), F32),
            vm((H, 8, N), F32),
            vm((H, T, T), BF),
            vm((T, T), BF),
            vm((H, PS, T), F32),
            vm((H, PS, T), BF),
            vm((H, 2 * PS, T), BF),
            vm((H, 2 * PS, T), BF),
            vm((T, T), F32),
            vm((N, T), F32),
            vm((N, T), F32),
            vm((T, N), BF),
            vm((T, N), BF),
            st, st, st, st, st, st, st, st,
            vm((INNER, T), BF),
            vm((T, INNER), BF),
            vm((INNER, T), BF),
            vm((T, COLS), BF),
            vm((T, COLS), BF),
            vm((6, 32, 16, CW), F32),
            vm((6, 63, 16, CW), BF),
            vm((6, 63, 16, CW), BF),
            dma((5,)),
            dma((SUB,)),
            dma((SUB,)),
            dma((3, SUB)),
            dma((3, SUB)),
            dma((4, SUB)),
            dma((4, SUB)),
            dma((3,)),
            dma((3,)),
            dma((4, 32)),
            dma((4, 32)),
            dma((32,)),
            dma((32,)),
            dma((6, 6)),
            dma((6, 6)),
        ],
        compiler_params=pltpu.CompilerParams(
            collective_id=0, has_side_effects=True, vmem_limit_bytes=60 * 1024 * 1024
        ),
    )(tokens[0], w_in, log_decay[0], grad_out[0])
    return out[None], gt[None], gw


def solution(mesh):
    return jax.shard_map(
        on_device,
        mesh=mesh,
        in_specs=(
            P("fsdp", "seq", None),
            P("fsdp", None),
            P("fsdp", None, "seq"),
            P("fsdp", "seq", None),
        ),
        out_specs=(P("fsdp", "seq", None), P("fsdp", "seq", None), P(("seq", "fsdp"), None)),
        check_vma=False,
    )
```

time: 225 us -> 141 us (0.63)
  Pallas kernels: 197 us -> 136 us
  matrix products: 11.4 us -> 0 us
  local copies, waits for them, and re-layouts: 15.3 us -> 4.04 us
    pallas_call x3 -> x1, Pallas kernels: 197 us -> 136 us  [on_device(): pl.pallas_call(kernel, name='mixer_step', out_shape=(jax.ShapeDtypeStruct...]
    dot_general x2 -> x0, matrix products: 11.4 us -> none  [mm(): return lax.dot_general(a, b, dims, preferred_element_type=F32)]
    unnamed x21 -> x7, local copies, waits for them, and re-layouts: 10.8 us -> 4.04 us
where the time goes in v2:
time: 141 us
  Pallas kernels  136 us (96%)
  local copies, waits for them, and re-layouts  4.04 us (3%)
    pallas_call x1, Pallas kernels, on_device(): pl.pallas_call(kernel, name='mixer_step', out_shape=(jax.ShapeDtypeStruct...  136 us
    unnamed x7, local copies, waits for them, and re-layouts  4.04 us

profile of v2, /device:TPU:0, one launch (start us, length us, event | category | flops | bytes accessed | tf_op | source)
XLA Modules:
  0.0 140.7 jit_solution(5746731233529028771)
XLA Ops:
  0.6 136.0 %mixer_step.1 = (bf16[256,2048]{1,0:T(8,128)(2,1)}, bf16[256,2048]{1,0:T(8,128)(2,1)}, f32[16,2304]{1,0:T(8,128)}) custom-call(bf16[256,2048]{1,0:T(8,128)(2,1)} %bitcast.5, bf16[512,2304]{1,0:T(8,128)(2,1)} %w_hbm.1, f32[32,256]{1,0:T(8,128)} %bitcast.9, bf16[256,2048]{1,0:T(8,128)(2,1)} %bitcast.6), custom_call_target="tpu_custom_call" | custom-call | tf_op jit(solution)/shard_map/mixer_step/pallas_call | solution.py:475
  136.6 0.0 copy-start
  136.6 0.0 copy-start.1
  136.7 2.4 %copy.10 = bf16[1,256,2048]{2,1,0:T(8,128)(2,1)} copy(bf16[1,256,2048]{2,1,0:T(8,128)(2,1)} %bitcast.8) | data formatting | bytes 2097152
  139.1 0.0 copy-done
  139.1 1.0 copy.11
  140.0 0.0 copy-done.1
  140.0 0.7 copy.12
Async XLA Ops:
  136.6 2.4 %copy-start = (bf16[256,2048]{1,0:T(8,128)(2,1)S(1)}, bf16[256,2048]{1,0:T(8,128)(2,1)}, u32[]{:S(2)}) copy-start(bf16[256,2048]{1,0:T(8,128)(2,1)} %get-tuple-element.7) | copy-start | bytes 3145732
  136.6 3.4 %copy-start.1 = (f32[16,2304]{1,0:T(8,128)S(1)}, f32[16,2304]{1,0:T(8,128)}, u32[]{:S(2)}) copy-start(f32[16,2304]{1,0:T(8,128)} %get-tuple-element.14) | copy-start | bytes 442372

commit v3 on v2

v3 whole, which is shorter than its diff:
```python
import functools
import jax
import jax.numpy as jnp
from jax import lax
from jax.experimental import pallas as pl
from jax.experimental.pallas import tpu as pltpu
from jax.sharding import PartitionSpec as P

BF = jnp.bfloat16
F32 = jnp.float32
EPS = 1e-5
H, PS, N, T, D, INNER, COLS = 32, 64, 128, 256, 2048, 2048, 2304
MESH = pl.DeviceIdType.MESH
NN = (((1,), (0,)), ((), ()))
NT = (((1,), (1,)), ((), ()))
TN = (((0,), (0,)), ((), ()))
CW = COLS // 6
OFF = [0, 32, 48, 56, 60, 62]
PIECES = 9


def mm(a, b, dims):
    return lax.dot_general(a, b, dims, preferred_element_type=F32)


def place():
    s = lax.axis_index("seq")
    f = lax.axis_index("fsdp")
    return s % 4, (s // 4) % 4, s // 16, f // 2, f % 2


def device(x, y, zl, zh, core):
    return (zl * 16 + y * 4 + x, zh * 2 + core)


def flip(dim, x, y, zl, zh):
    if dim == 0:
        x = x + 1 - 2 * (x % 2)
    elif dim == 1:
        x = 3 - x
    elif dim == 2:
        y = y + 1 - 2 * (y % 2)
    elif dim == 3:
        y = 3 - y
    elif dim == 4:
        zl = 1 - zl
    else:
        zl, zh = 1 - zl, 1 - zh
    return x, y, zl, zh


def order(color):
    dims = [(color + k) % 6 for k in range(6)]
    found = []
    for i in range(64):
        r = 0
        for k in range(6):
            if (i >> (5 - k)) & 1:
                r |= 1 << dims[k]
        found.append(r)
    return found


def remote(src, dst, ssem, rsem, to):
    return pltpu.make_async_remote_copy(src, dst, ssem, rsem, to, MESH)


def kernel(
    tok_hbm, w_hbm, log_ref, go_hbm,
    out_hbm, gt_hbm, gw_ref,
    wf, tok, tokt, ts, ta, tb, go, gtr, xt, rows, tot, tin,
    dec, aff, y, gm, gmw, xs, gaff, dct, dbt, bmat, cmat,
    up1, in1, down1, ent, up2, in2, down2, adj,
    outt, outn, grad, g, gs, part, sb, rb,
    lsem, far_s, far_r, nb_s, nb_r, sf_s, sf_r, sib_s, sib_r, gsib_s, gsib_r,
    ssem, rsem, tsem, wsem, wrsem,
):
    s = lax.axis_index("seq")
    f = lax.axis_index("fsdp")
    x, y_, zl, zh, core = place()
    here = (x, y_, zl, zh)
    sib = device(*here, 1 - core)
    far = device(*flip(5, *here), core)
    peers = [device(*flip(d, *here), core) for d in range(6)]
    barrier = pltpu.get_barrier_semaphore()

    def peer(o, sign=1):
        px = lax.rem(x + 4 + sign * (o % 4), 4)
        py = lax.rem(y_ + 4 + sign * ((o // 4) % 4), 4)
        pz = lax.rem(zl + o // 16, 2)
        return pz * 16 + py * 4 + px

    @pl.loop(1, 32)
    def _(o):
        pl.semaphore_signal(barrier, inc=1, device_id=(peer(o), f), device_id_type=MESH)

    def across(dims):
        p = here
        for d in dims:
            p = flip(d, *p)
        return device(*p, core)

    further = [(3, 5), (4, 5), (3, 4, 5), (0, 5), (0, 4, 5), (1, 5), (0, 1, 5)]
    greeted = [sib, far] + [across(d) for d in further]
    for q in greeted:
        pl.semaphore_signal(barrier, inc=1, device_id=q, device_id_type=MESH)

    def whole(i):
        return pl.ds(pl.multiple_of(i * 512, 512), 512)

    tok_in = pltpu.make_async_copy(tok_hbm, tok, lsem.at[0])
    go_in = pltpu.make_async_copy(go_hbm, go, lsem.at[1])
    own_in = pltpu.make_async_copy(w_hbm, wf.at[whole(f)], lsem.at[2])
    tok_in.start()
    own_in.start()
    go_in.start()

    ri = lax.broadcasted_iota(jnp.int32, (T, T), 0)
    ci = lax.broadcasted_iota(jnp.int32, (T, T), 1)
    log = log_ref[...]
    cum = lax.dot_general(
        log, (ri <= ci).astype(F32), NN, precision=lax.Precision.HIGHEST, preferred_element_type=F32
    )
    exc = cum - log
    last = cum[:, T - 1 : T]
    cumt = cum.T
    exct = exc.T
    fac = (jnp.exp(cum), jnp.exp(last - exc), jnp.exp(last - cum), jnp.exp(exc))
    lastb = jnp.broadcast_to(last, (H, N))
    for h in range(H):
        for k in range(4):
            rows[h, k : k + 1, :] = fac[k][h : h + 1, :]
    for h in range(8):
        four = [lastb[8 * k + h : 8 * k + h + 1, :] for k in range(4)]
        v = jnp.concatenate(four + four, axis=0)
        for k in range(4):
            tot[4 * h + k] = v

    pl.semaphore_wait(barrier, 31 + len(greeted))

    far_f = (1 - zh) * 2 + core
    sibfar_f = (1 - zh) * 2 + 1 - core
    q0, q1 = (x + zl) % 2, (y_ + zl) % 2
    colour = q0 + 2 * q1
    others = [(1 - q0) + 2 * q1, q0 + 2 * (1 - q1), (1 - q0) + 2 * (1 - q1)]
    ndims = [0, 2, 4]

    def piece(shard, quarter, i):
        r = pl.ds(pl.multiple_of(shard * 512 + quarter * 128, 128), 128)
        return r, pl.ds(256 * ((i + 8) % 9), 256)

    def far_copy(i):
        mine = pl.ds(pl.multiple_of(others[2] * 128, 128), 128)
        p = piece(f, others[2], i)
        return remote(w_hbm.at[mine, p[1]], wf.at[p], far_s.at[i], far_r.at[i], far)

    def near_copy(d, i):
        p = piece(far_f, colour, i)
        return remote(wf.at[p], wf.at[p], nb_s.at[d, i], nb_r.at[d, i], peers[ndims[d]])

    def pass_copy(j, i):
        p = piece(far_f, colour if j == 0 else others[j - 1], i)
        return remote(wf.at[p], wf.at[p], sf_s.at[j, i], sf_r.at[j, i], sib)

    own_out = remote(w_hbm, wf.at[whole(f)], sib_s.at[0], sib_r.at[0], sib)
    for i in range(PIECES):
        far_copy(i).start()
    own_out.start()

    def tot_copy(o):
        p = peer(o)
        return remote(tot.at[p], tin.at[s], tsem.at[0], tsem.at[1], (p, f))

    @pl.loop(1, 32)
    def _(o):
        tot_copy(o).start()

    tin[s] = tot[s]
    most = pl.ds(0, 31)

    diag = ri == ci

    def decays(h):
        a = cum[h : h + 1, :] - cumt[:, h : h + 1]
        b = exct[:, h : h + 1] - exc[h : h + 1, :]
        e = jnp.exp(jnp.minimum(a, b))
        dec[h] = jnp.where(diag, 2.0, e).astype(BF)

    tok_in.wait()
    for c in range(16):
        tt = tok[:, 128 * c : 128 * c + 128].T
        for k in range(8):
            b = 8 * c + k
            tokt[b % 2, b // 2] = tt[16 * k : 16 * k + 16, :]
    tok_out = remote(tokt.at[1 - core], ts, sib_s.at[1], sib_r.at[1], sib)
    tok_out.start()

    go_in.wait()
    for c in range(16):
        gtr[128 * c : 128 * c + 128, :] = go[:, 128 * c : 128 * c + 128].T

    def head(h):
        return pl.ds(pl.multiple_of(h * PS, PS), PS)

    def transfer(k, q, p):
        src, dst = ((up1, in1), (down1, ent), (up2, in2), (down2, adj))[k]
        a = src.at[q, p] if k % 2 else src.at[q, :, p]
        b = dst.at[q, :, s] if k % 2 else dst.at[q, s]
        return remote(a, b, ssem.at[k, q], rsem.at[k, q], (p, f))

    def send(k, q):
        src, dst = ((up1, in1), (down1, ent), (up2, in2), (down2, adj))[k]

        @pl.loop(1, 32)
        def _(o):
            transfer(k, q, peer(o)).start()

        if k % 2:
            dst[q, :, s] = src[q, s]
        else:
            dst[q, s] = src[q, :, s]

    def whole_chunk(k, q):
        src, dst = ((up1, in1), (down1, ent), (up2, in2), (down2, adj))[k]
        a = src.at[q, most] if k % 2 else src.at[q, :, most]
        b = dst.at[q, :, most] if k % 2 else dst.at[q, most]
        return a, b

    def arrived(k, q):
        _, b = whole_chunk(k, q)
        remote(b, b, ssem.at[k, q], rsem.at[k, q], sib).wait_recv()

    def left(k, q):
        a, _ = whole_chunk(k, q)
        remote(a, a, ssem.at[k, q], rsem.at[k, q], sib).wait_send()

    def pairs(q, body):
        @pl.loop(0, 4)
        def _(t):
            body([(8 * q + 2 * t + i, 2 * t + i) for i in range(2)])

    def quarter(ref, q, i):
        return jnp.concatenate(
            [ref[q, k, pl.ds(4 * i, 4)].reshape(PS, N) for k in range(2)], axis=0
        )

    def store(ref, q, i, v):
        v = v.reshape(2, 4, 16, N)
        for k in range(2):
            ref[q, k, pl.ds(4 * i, 4)] = v[k]

    ctall = pl.ds(INNER + N, N)
    btall = pl.ds(INNER, N)

    def project(q):
        cols = pl.ds(512 * q, 512)
        v = mm(tok[...], wf[:, cols], NN).astype(BF)
        for c in range(4):
            xt[512 * q + 128 * c : 512 * q + 128 * c + 128, :] = v[:, 128 * c : 128 * c + 128].T

    def project_last():
        v = mm(tok[...], wf[:, INNER:COLS], NN).astype(BF)
        bmat[...] = v[:, :N]
        cmat[...] = v[:, N:]
        xt[btall, :] = v[:, :N].T
        xt[ctall, :] = v[:, N:].T
        aff[...] = mm(v[:, :N], xt[ctall, :], NN).astype(BF)

    def states(q):
        def body(hs):
            for h, i in hs:
                xv = xt[head(h), :].astype(F32)
                r = rows[h]
                xs[h, pl.ds(0, PS), :] = (xv * r[2:3, :]).astype(BF)
                xs[h, pl.ds(PS, PS), :] = (xv * r[3:4, :]).astype(BF)
            for h, i in hs:
                store(up1, q, i, mm(xs[h], bmat[...], NN).astype(BF))

        pairs(q, body)
        send(0, q)

    def local_forward(q):
        def body(hs):
            for h, _ in hs:
                y[h] = mm(xt[head(h), :], aff[...] * dec[h], NN)

        pairs(q, body)

    def scan(k, q, fwd, rev):
        src, dst = ((in1, down1), None, (in2, down2))[k]
        arrived(k, q)

        def one(i, carry):
            a, b = carry
            j = 31 - i
            dst[q, i, fwd] = a.astype(BF)
            dst[q, j, rev] = b.astype(BF)
            a = tin[i, q : q + 1, :] * a + src[q, i, fwd].astype(F32)
            b = tin[j, q : q + 1, :] * b + src[q, j, rev].astype(F32)
            return a, b

        zero = jnp.zeros((16, N), F32)
        lax.fori_loop(0, 32, one, (zero, zero), unroll=4)
        send(k + 1, q)

    def mixture(q):
        arrived(1, q)

        def body(hs):
            for h, i in hs:
                r = rows[h]
                car = mm(quarter(ent, q, i), xt[ctall, :], NN)
                mix = y[h] + r[0:1, :] * car[:PS] + r[1:2, :] * car[PS:]
                ms = jnp.sum(mix * mix, axis=0, keepdims=True) * (1.0 / PS)
                inv = 1.0 / jnp.sqrt(ms + EPS)
                z = mix * inv
                outt[head(h), :] = z.astype(BF)
                gv = gtr[head(h), :].astype(F32)
                m = jnp.sum(gv * z, axis=0, keepdims=True) * (1.0 / PS)
                gr = (gv - z * m) * inv
                gm[h] = gr.astype(BF)
                gmw[h, pl.ds(0, PS), :] = (gr * r[0:1, :]).astype(BF)
                gmw[h, pl.ds(PS, PS), :] = (gr * r[1:2, :]).astype(BF)
            for h, i in hs:
                store(up2, q, i, mm(gmw[h], cmat[...], NN).astype(BF))

        pairs(q, body)
        send(2, q)

    def local_backward(q):
        def body(hs):
            total = None
            for h, i in hs:
                d = dec[h]
                gh = gm[h]
                y[h] = mm(gh, aff[...] * d, NT)
                gw = mm(xt[head(h), :], gh, TN) * d.astype(F32)
                total = gw if total is None else total + gw
            gaff[...] += total
            e = jnp.concatenate([quarter(ent, q, i) for _, i in hs], axis=0)
            w = jnp.concatenate([gmw[h] for h, _ in hs], axis=0)
            dct[...] += mm(e, w, TN)

        pairs(q, body)

    def finish(q):
        arrived(3, q)

        def body(hs):
            total = None
            for h, i in hs:
                r = rows[h]
                e = quarter(adj, q, i)
                car = mm(e, xt[btall, :], NN)
                gx = y[h] + r[2:3, :] * car[:PS] + r[3:4, :] * car[PS:]
                grad[head(h), :] = gx.astype(BF)
                v = mm(e, xs[h], TN)
                total = v if total is None else total + v
            dbt[...] += total

        pairs(q, body)
        for c in range(4 * q, 4 * q + 4):
            g[:, 128 * c : 128 * c + 128] = grad[128 * c : 128 * c + 128, :].T
        g_copy(q).start()

    def g_copy(q):
        cols = pl.ds(512 * q, 512 if q < 4 else 256)
        return remote(g.at[:, cols], gs.at[:, cols], gsib_s.at[q], gsib_r.at[q], sib)

    todo = list(range(H))

    def some(n):
        for h in todo[:n]:
            decays(h)
        del todo[:n]

    gaff[...] = jnp.zeros_like(gaff)
    dct[...] = jnp.zeros_like(dct)
    dbt[...] = jnp.zeros_like(dbt)
    some(6)
    for i in range(PIECES + 2):
        if i < PIECES:
            far_copy(i).wait_recv()
            for d in range(3):
                near_copy(d, i).start()
            pass_copy(0, i).start()
        if 1 <= i <= PIECES:
            for d in range(3):
                p = piece(far_f, others[d], i - 1)
                remote(
                    wf.at[p], wf.at[p], nb_s.at[d, i - 1], nb_r.at[d, i - 1], peers[ndims[d]]
                ).wait_recv()
                pass_copy(1 + d, i - 1).start()
        if i >= 2:
            for j in range(4):
                p = piece(sibfar_f, colour if j == 0 else others[j - 1], i - 2)
                remote(wf.at[p], wf.at[p], sf_s.at[j, i - 2], sf_r.at[j, i - 2], sib).wait_recv()
            if i == 2:
                own_in.wait()
                own_out.wait_recv()
                project_last()
            elif i % 2 == 0:
                project(i // 2 - 2)
                states(i // 2 - 2)
        if i not in (2, 4, 6, 8, 10):
            some(6)
    some(H)
    local_forward(0)
    local_forward(1)
    remote(
        tin.at[most], tin.at[most], tsem.at[0], tsem.at[1], sib
    ).wait_recv()
    tin[...] = jnp.exp(tin[...])

    def block(r):
        p = here
        for d in range(6):
            if (r >> d) & 1:
                p = flip(d, *p)
        return p[2] * 32 + p[1] * 8 + p[0] * 2 + p[3]

    def relay_tokens():
        tok_out.wait_recv()
        for r in range(64):
            b = block(r)
            ta[r] = tokt[core, b]
            tb[r] = ts[b]

    out_copy = pltpu.make_async_copy(outn, out_hbm, lsem.at[3])

    def give_output():
        for c in range(16):
            outn[:, 128 * c : 128 * c + 128] = outt[128 * c : 128 * c + 128, :].T
        out_copy.start()

    def close_affinity():
        ga = gaff[...].astype(BF)
        dct[...] += mm(xt[btall, :], ga, NN)
        dbt[...] += mm(xt[ctall, :], ga, NT)
        g[:, INNER + N : COLS] = dct[...].astype(BF).T

    def product(c, half):
        ids = order(c)[32 * half : 32 * half + 32]
        la = jnp.concatenate([ta[r] for r in ids], axis=0)
        lb = jnp.concatenate([tb[r] for r in ids], axis=0)
        cols = pl.ds(c * CW, CW)
        v = mm(la, g[:, cols], NN) + mm(lb, gs[:, cols], NN)
        return v.reshape(32, 16, CW).astype(BF)

    def halve(c, k):
        p = pl.ds(OFF[k], 32 >> k)
        return remote(sb.at[c, p], rb.at[c, p], wsem.at[c, k], wrsem.at[c, k], peers[(c + k) % 6])

    def direct(c, i):
        dims = [(c + 3 + b) % 6 for b in range(3) if (i >> (2 - b)) & 1]
        return remote(
            part.at[c, i], rb.at[c, OFF[3] + i - 1], wsem.at[c, 3], wrsem.at[c, 3], across(dims)
        )

    def first(c):
        sb[c, pl.ds(0, 32)] = product(c, 1)
        halve(c, 0).start()

    def tokens_part(i):
        r = pl.ds(512 * i, 512)
        tok[:, r] = mm(g[...], wf[r, :], NT).astype(BF)

    scan(0, 0, 0, 1)
    scan(0, 1, 0, 1)
    local_forward(2)
    scan(0, 2, 0, 1)
    mixture(0)
    local_forward(3)
    scan(0, 3, 0, 1)
    mixture(1)
    local_backward(0)
    mixture(2)
    scan(2, 0, 1, 0)
    local_backward(1)
    mixture(3)
    scan(2, 1, 1, 0)
    local_backward(2)
    give_output()
    scan(2, 2, 1, 0)
    local_backward(3)
    relay_tokens()
    finish(0)
    scan(2, 3, 1, 0)
    close_affinity()
    finish(1)
    g_copy(0).wait_recv()
    first(0)
    finish(2)
    g_copy(1).wait_recv()
    first(1)
    finish(3)
    g[:, INNER : INNER + N] = dbt[...].astype(BF).T
    g_copy(4).start()
    g_copy(2).wait_recv()
    first(2)
    first(3)
    g_copy(3).wait_recv()
    first(4)
    g_copy(4).wait_recv()
    first(5)
    for c in range(6):
        part[c] = product(c, 0)
    tokens_part(0)
    tokens_part(1)
    tokens_part(2)
    tokens_part(3)
    gt_copy = pltpu.make_async_copy(tok, gt_hbm, lsem.at[4])
    gt_copy.start()
    for k in range(1, 4):
        n = 64 >> k
        m = n // 2
        for c in range(6):
            halve(c, k - 1).wait_recv()
            if k < 3:
                sb[c, pl.ds(OFF[k], m)] = part[c, pl.ds(m, m)] + rb[c, pl.ds(OFF[k - 1] + m, m)]
                halve(c, k).start()
            else:
                part[c, pl.ds(0, n)] += rb[c, pl.ds(OFF[k - 1], n)]
                for i in range(7, 0, -1):
                    direct(c, i).start()
        if k < 3:
            for c in range(6):
                part[c, pl.ds(0, m)] += rb[c, pl.ds(OFF[k - 1], m)]
    rest = pl.ds(OFF[3], 7)
    for c in range(6):
        remote(rb.at[c, rest], rb.at[c, rest], wsem.at[c, 3], wrsem.at[c, 3], sib).wait_recv()
        v = part[c, 0].astype(F32)
        for i in range(7):
            v = v + rb[c, OFF[3] + i].astype(F32)
        gw_ref[:, pl.ds(c * CW, CW)] = v

    for i in range(PIECES):
        far_copy(i).wait_send()
        for d in range(3):
            near_copy(d, i).wait_send()
        for j in range(4):
            pass_copy(j, i).wait_send()
    own_out.wait_send()
    tok_out.wait_send()
    remote(tot.at[most], tot.at[most], tsem.at[0], tsem.at[1], sib).wait_send()
    for q in range(4):
        for k in range(4):
            left(k, q)
    for q in range(5):
        g_copy(q).wait_send()
    for c in range(6):
        for k in range(3):
            halve(c, k).wait_send()
        sent = pl.ds(1, 7)
        remote(
            part.at[c, sent], part.at[c, sent], wsem.at[c, 3], wrsem.at[c, 3], sib
        ).wait_send()
    out_copy.wait()
    gt_copy.wait()


def on_device(tokens, w_in, log_decay, grad_out):
    v = pl.BlockSpec(memory_space=pltpu.VMEM)
    a = pl.BlockSpec(memory_space=pl.ANY)
    vm = pltpu.VMEM
    st = vm((4, 2, 32, 16, N), BF)
    sr = vm((4, 32, 2, 16, N), BF)
    dma = pltpu.SemaphoreType.DMA
    out, gt, gw = pl.pallas_call(
        kernel,
        name="mixer_step",
        out_shape=(
            jax.ShapeDtypeStruct((T, INNER), BF),
            jax.ShapeDtypeStruct((T, D), BF),
            jax.ShapeDtypeStruct((16, COLS), F32),
        ),
        in_specs=[a, a, v, a],
        out_specs=(a, a, v),
        scratch_shapes=[
            vm((D, COLS), BF),
            vm((T, D), BF),
            vm((2, 64, 16, T), BF),
            vm((64, 16, T), BF),
            vm((64, 16, T), BF),
            vm((64, 16, T), BF),
            vm((T, INNER), BF),
            vm((INNER, T), BF),
            vm((COLS, T), BF),
            vm((H, 8, T), F32),
            vm((H, 8, N), F32),
            vm((H, 8, N), F32),
            vm((H, T, T), BF),
            vm((T, T), BF),
            vm((H, PS, T), F32),
            vm((H, PS, T), BF),
            vm((H, 2 * PS, T), BF),
            vm((H, 2 * PS, T), BF),
            vm((T, T), F32),
            vm((N, T), F32),
            vm((N, T), F32),
            vm((T, N), BF),
            vm((T, N), BF),
            st, sr, sr, st, st, sr, sr, st,
            vm((INNER, T), BF),
            vm((T, INNER), BF),
            vm((INNER, T), BF),
            vm((T, COLS), BF),
            vm((T, COLS), BF),
            vm((6, 32, 16, CW), BF),
            vm((6, 63, 16, CW), BF),
            vm((6, 63, 16, CW), BF),
            dma((5,)),
            dma((PIECES,)),
            dma((PIECES,)),
            dma((3, PIECES)),
            dma((3, PIECES)),
            dma((4, PIECES)),
            dma((4, PIECES)),
            dma((2,)),
            dma((2,)),
            dma((5,)),
            dma((5,)),
            dma((4, 4)),
            dma((4, 4)),
            dma((2,)),
            dma((6, 4)),
            dma((6, 4)),
        ],
        compiler_params=pltpu.CompilerParams(
            collective_id=0, has_side_effects=True, vmem_limit_bytes=60 * 1024 * 1024
        ),
    )(tokens[0], w_in, log_decay[0], grad_out[0])
    return out[None], gt[None], gw


def solution(mesh):
    return jax.shard_map(
        on_device,
        mesh=mesh,
        in_specs=(
            P("fsdp", "seq", None),
            P("fsdp", None),
            P("fsdp", None, "seq"),
            P("fsdp", "seq", None),
        ),
        out_specs=(P("fsdp", "seq", None), P("fsdp", "seq", None), P(("seq", "fsdp"), None)),
        check_vma=False,
    )
```

time: 141 us -> 123 us (0.87)
  Pallas kernels: 136 us -> 118 us
    pallas_call x1, Pallas kernels: 136 us -> 118 us  [on_device(): pl.pallas_call(kernel, name='mixer_step', out_shape=(jax.ShapeDtypeStruct...]
where the time goes in v3:
time: 123 us; the launch traced here: 122 us
  Pallas kernels  118 us (96%)
  local copies, waits for them, and re-layouts  4.04 us (3%)
    pallas_call x1, Pallas kernels, on_device(): pl.pallas_call(kernel, name='mixer_step', out_shape=(jax.ShapeDtypeStruct...  118 us
    unnamed x7, local copies, waits for them, and re-layouts  4.04 us

profile of v3, /device:TPU:0, one launch (start us, length us, event | category | flops | bytes accessed | tf_op | source)
XLA Modules:
  0.0 122.5 jit_solution(2194742557177539185)
XLA Ops:
  0.6 117.8 %mixer_step.1 = (bf16[256,2048]{1,0:T(8,128)(2,1)}, bf16[256,2048]{1,0:T(8,128)(2,1)}, f32[16,2304]{1,0:T(8,128)}) custom-call(bf16[256,2048]{1,0:T(8,128)(2,1)} %bitcast.5, bf16[512,2304]{1,0:T(8,128)(2,1)} %w_hbm.1, f32[32,256]{1,0:T(8,128)} %bitcast.9, bf16[256,2048]{1,0:T(8,128)(2,1)} %bitcast.6), custom_call_target="tpu_custom_call" | custom-call | tf_op jit(solution)/shard_map/mixer_step/pallas_call | solution.py:569
  118.4 0.0 copy-start
  118.4 0.0 copy-start.1
  118.4 2.4 %copy.10 = bf16[1,256,2048]{2,1,0:T(8,128)(2,1)} copy(bf16[1,256,2048]{2,1,0:T(8,128)(2,1)} %bitcast.8) | data formatting | bytes 2097152
  120.8 0.0 copy-done
  120.8 1.0 copy.11
  121.8 0.0 copy-done.1
  121.8 0.7 copy.12
Async XLA Ops:
  118.4 2.4 %copy-start = (bf16[256,2048]{1,0:T(8,128)(2,1)S(1)}, bf16[256,2048]{1,0:T(8,128)(2,1)}, u32[]{:S(2)}) copy-start(bf16[256,2048]{1,0:T(8,128)(2,1)} %get-tuple-element.7) | copy-start | bytes 3145732
  118.4 3.4 %copy-start.1 = (f32[16,2304]{1,0:T(8,128)S(1)}, f32[16,2304]{1,0:T(8,128)}, u32[]{:S(2)}) copy-start(f32[16,2304]{1,0:T(8,128)} %get-tuple-element.14) | copy-start | bytes 442372

commit v4 on v3

--- a/solution.py
+++ b/solution.py
@@ -17,6 +17,7 @@
 CW = COLS // 6
 OFF = [0, 32, 48, 56, 60, 62]
 PIECES = 9
+GROUP = 4
 
 
 def mm(a, b, dims):
@@ -235,9 +236,9 @@
         remote(a, a, ssem.at[k, q], rsem.at[k, q], sib).wait_send()
 
     def pairs(q, body):
-        @pl.loop(0, 4)
+        @pl.loop(0, 8 // GROUP)
         def _(t):
-            body([(8 * q + 2 * t + i, 2 * t + i) for i in range(2)])
+            body([(8 * q + GROUP * t + i, GROUP * t + i) for i in range(GROUP)])
 
     def quarter(ref, q, i):
         return jnp.concatenate(
@@ -300,7 +301,7 @@
             return a, b
 
         zero = jnp.zeros((16, N), F32)
-        lax.fori_loop(0, 32, one, (zero, zero), unroll=4)
+        lax.fori_loop(0, 32, one, (zero, zero), unroll=32)
         send(k + 1, q)
 
     def mixture(q):
@@ -377,33 +378,67 @@
     gaff[...] = jnp.zeros_like(gaff)
     dct[...] = jnp.zeros_like(dct)
     dbt[...] = jnp.zeros_like(dbt)
-    some(6)
-    for i in range(PIECES + 2):
-        if i < PIECES:
-            far_copy(i).wait_recv()
-            for d in range(3):
-                near_copy(d, i).start()
-            pass_copy(0, i).start()
-        if 1 <= i <= PIECES:
-            for d in range(3):
-                p = piece(far_f, others[d], i - 1)
-                remote(
-                    wf.at[p], wf.at[p], nb_s.at[d, i - 1], nb_r.at[d, i - 1], peers[ndims[d]]
-                ).wait_recv()
-                pass_copy(1 + d, i - 1).start()
-        if i >= 2:
-            for j in range(4):
-                p = piece(sibfar_f, colour if j == 0 else others[j - 1], i - 2)
-                remote(wf.at[p], wf.at[p], sf_s.at[j, i - 2], sf_r.at[j, i - 2], sib).wait_recv()
-            if i == 2:
-                own_in.wait()
-                own_out.wait_recv()
-                project_last()
-            elif i % 2 == 0:
-                project(i // 2 - 2)
-                states(i // 2 - 2)
-        if i not in (2, 4, 6, 8, 10):
-            some(6)
+    def from_far(i):
+        far_copy(i).wait_recv()
+        for d in range(3):
+            near_copy(d, i).start()
+        pass_copy(0, i).start()
+
+    def from_near(i):
+        for d in range(3):
+            p = piece(far_f, others[d], i)
+            remote(
+                wf.at[p], wf.at[p], nb_s.at[d, i], nb_r.at[d, i], peers[ndims[d]]
+            ).wait_recv()
+            pass_copy(1 + d, i).start()
+
+    def from_sibling(i):
+        for j in range(4):
+            p = piece(sibfar_f, colour if j == 0 else others[j - 1], i)
+            remote(wf.at[p], wf.at[p], sf_s.at[j, i], sf_r.at[j, i], sib).wait_recv()
+
+    some(8)
+    from_far(0)
+    some(8)
+    from_far(1)
+    some(4)
+    from_near(0)
+    from_far(2)
+    some(4)
+    from_near(1)
+    from_far(3)
+    from_sibling(0)
+    own_in.wait()
+    own_out.wait_recv()
+    project_last()
+    from_near(2)
+    from_far(4)
+    from_sibling(1)
+    from_sibling(2)
+    from_near(3)
+    from_far(5)
+    project(0)
+    from_near(4)
+    from_far(6)
+    from_sibling(3)
+    states(0)
+    from_near(5)
+    from_far(7)
+    from_far(8)
+    from_sibling(4)
+    project(1)
+    from_near(6)
+    states(1)
+    from_near(7)
+    from_near(8)
+    from_sibling(5)
+    from_sibling(6)
+    project(2)
+    states(2)
+    from_sibling(7)
+    from_sibling(8)
+    project(3)
+    states(3)
     some(H)
     local_forward(0)
     local_forward(1)
@@ -522,7 +557,11 @@
             else:
                 part[c, pl.ds(0, n)] += rb[c, pl.ds(OFF[k - 1], n)]
                 for i in range(7, 0, -1):
-                    direct(c, i).start()
+                    if c > 0:
+                        direct(c - 1, i).start()
+        if k == 3:
+            for i in range(7, 0, -1):
+                direct(5, i).start()
         if k < 3:
             for c in range(6):
                 part[c, pl.ds(0, m)] += rb[c, pl.ds(OFF[k - 1], m)]
@@ -557,6 +596,29 @@
         ).wait_send()
     out_copy.wait()
     gt_copy.wait()
+
+
+def settle_kernel(a, b, c, a2, b2, c2):
+    a2[...] = a[...]
+    b2[...] = b[...]
+    c2[...] = c[...]
+
+
+def settle(*arrays):
+    specs = [
+        pl.BlockSpec((1, T // 2, INNER), lambda i: (0, i, 0)),
+        pl.BlockSpec((1, T // 2, D), lambda i: (0, i, 0)),
+        pl.BlockSpec((16, COLS // 2), lambda i: (0, i)),
+    ]
+    return pl.pallas_call(
+        settle_kernel,
+        name="settle",
+        grid=(2,),
+        out_shape=tuple(jax.ShapeDtypeStruct(v.shape, v.dtype) for v in arrays),
+        in_specs=specs,
+        out_specs=tuple(specs),
+        compiler_params=pltpu.CompilerParams(vmem_limit_bytes=60 * 1024 * 1024),
+    )(*arrays)
 
 
 def on_device(tokens, w_in, log_decay, grad_out):
@@ -630,7 +692,7 @@
             collective_id=0, has_side_effects=True, vmem_limit_bytes=60 * 1024 * 1024
         ),
     )(tokens[0], w_in, log_decay[0], grad_out[0])
-    return out[None], gt[None], gw
+    return settle(out[None], gt[None], gw)
 
 
 def solution(mesh):

time: 123 us -> 117 us (0.951)
  local copies, waits for them, and re-layouts: 4.04 us -> 0 us
  Pallas kernels: 118 us -> 116 us
    pallas_call x1, Pallas kernels: 118 us -> 113 us  [on_device(): pl.pallas_call(kernel, name='mixer_step', out_shape=(jax.ShapeDtypeStruct...]
    unnamed x7 -> x0, local copies, waits for them, and re-layouts: 4.04 us -> none
    pallas_call x0 -> x1, Pallas kernels: none -> 2.64 us  [settle(): pl.pallas_call(settle_kernel, name='settle', grid=(2,), out_shape=tuple((...]
where the time goes in v4:
time: 117 us; the launch traced here: 116 us
  Pallas kernels  116 us (99%)
    pallas_call x1, Pallas kernels, on_device(): pl.pallas_call(kernel, name='mixer_step', out_shape=(jax.ShapeDtypeStruct...  113 us
    pallas_call x1, Pallas kernels, settle(): pl.pallas_call(settle_kernel, name='settle', grid=(2,), out_shape=tuple((...  2.64 us

profile of v4, /device:TPU:0, one launch (start us, length us, event | category | flops | bytes accessed | tf_op | source)
XLA Modules:
  0.0 116.4 jit_solution(13588024021244451762)
XLA Ops:
  0.6 113.1 %mixer_step.1 = (bf16[256,2048]{1,0:T(8,128)(2,1)}, bf16[256,2048]{1,0:T(8,128)(2,1)}, f32[16,2304]{1,0:T(8,128)}) custom-call(bf16[256,2048]{1,0:T(8,128)(2,1)} %bitcast.5, bf16[512,2304]{1,0:T(8,128)(2,1)} %w_hbm.1, f32[32,256]{1,0:T(8,128)} %bitcast.9, bf16[256,2048]{1,0:T(8,128)(2,1)} %bitcast.6), custom_call_target="tpu_custom_call" | custom-call | tf_op jit(solution)/shard_map/mixer_step/pallas_call | solution.py:631
  113.7 2.6 %settle.1 = (bf16[1,256,2048]{2,1,0:T(8,128)(2,1)}, bf16[1,256,2048]{2,1,0:T(8,128)(2,1)}, f32[16,2304]{1,0:T(8,128)}) custom-call(bf16[1,256,2048]{2,1,0:T(8,128)(2,1)} %bitcast.7, bf16[1,256,2048]{2,1,0:T(8,128)(2,1)} %bitcast.8, f32[16,2304]{1,0:T(8,128)} %get-tuple-element.8.c), custom_call_target="tpu_custom_call" | custom-call | tf_op jit(solution)/shard_map/settle/pallas_call | solution.py:613

commit v5 on v4

--- a/solution.py
+++ b/solution.py
@@ -15,8 +15,10 @@
 NT = (((1,), (1,)), ((), ()))
 TN = (((0,), (0,)), ((), ()))
 CW = COLS // 6
-OFF = [0, 32, 48, 56, 60, 62]
+OFF = [0, 32, 48, 56]
+UNITS = [(c, 0, 256, 256 * c) for c in range(6)] + [(c, 256, 128, 1536 + 128 * c) for c in range(6)]
 PIECES = 9
+NEAR = 7
 GROUP = 4
 
 
@@ -51,7 +53,7 @@
 
 
 def order(color):
-    dims = [(color + k) % 6 for k in range(6)]
+    dims = [(color + 5 + k) % 6 for k in range(6)]
     found = []
     for i in range(64):
         r = 0
@@ -85,15 +87,14 @@
     peers = [device(*flip(d, *here), core) for d in range(6)]
     barrier = pltpu.get_barrier_semaphore()
 
-    def peer(o, sign=1):
-        px = lax.rem(x + 4 + sign * (o % 4), 4)
-        py = lax.rem(y_ + 4 + sign * ((o // 4) % 4), 4)
-        pz = lax.rem(zl + o // 16, 2)
-        return pz * 16 + py * 4 + px
-
-    @pl.loop(1, 32)
-    def _(o):
-        pl.semaphore_signal(barrier, inc=1, device_id=(peer(o), f), device_id_type=MESH)
+    pxs = [lax.rem(x + d, 4) for d in range(4)]
+    pys = [4 * lax.rem(y_ + d, 4) for d in range(4)]
+    pzs = [16 * lax.rem(zl + d, 2) for d in range(2)]
+    pyz = [a + b for a in pzs for b in pys]
+    ring = [pyz[o // 4] + pxs[o % 4] for o in range(1, 32)]
+
+    for p in ring:
+        pl.semaphore_signal(barrier, inc=1, device_id=(p, f), device_id_type=MESH)
 
     def across(dims):
         p = here
@@ -141,26 +142,40 @@
 
     far_f = (1 - zh) * 2 + core
     sibfar_f = (1 - zh) * 2 + 1 - core
-    q0, q1 = (x + zl) % 2, (y_ + zl) % 2
-    colour = q0 + 2 * q1
-    others = [(1 - q0) + 2 * q1, q0 + 2 * (1 - q1), (1 - q0) + 2 * (1 - q1)]
-    ndims = [0, 2, 4]
+    bits = [(x + x // 2) % 2, x // 2, (y_ + y_ // 2) % 2, y_ // 2, zl]
+
+    def cover(i):
+        dims = [(i + k) % 5 for k in range(3)]
+        v = [bits[d] for d in dims]
+        q0, q1 = (v[0] + v[2]) % 2, (v[1] + v[2]) % 2
+        theirs = [(1 - q0) + 2 * q1, q0 + 2 * (1 - q1), (1 - q0) + 2 * (1 - q1)]
+        mine = q0 + 2 * q1
+        return dims, mine, theirs, theirs[dims.index(4)] if 4 in dims else mine
+
+    covers = [cover(i) for i in range(PIECES)]
 
     def piece(shard, quarter, i):
         r = pl.ds(pl.multiple_of(shard * 512 + quarter * 128, 128), 128)
         return r, pl.ds(256 * ((i + 8) % 9), 256)
 
     def far_copy(i):
-        mine = pl.ds(pl.multiple_of(others[2] * 128, 128), 128)
-        p = piece(f, others[2], i)
+        if i >= NEAR:
+            cols = piece(f, 0, i)[1]
+            p = (whole(f), cols)
+            return remote(w_hbm.at[:, cols], wf.at[p], far_s.at[i], far_r.at[i], far)
+        quarter = covers[i][3]
+        mine = pl.ds(pl.multiple_of(quarter * 128, 128), 128)
+        p = piece(f, quarter, i)
         return remote(w_hbm.at[mine, p[1]], wf.at[p], far_s.at[i], far_r.at[i], far)
 
     def near_copy(d, i):
-        p = piece(far_f, colour, i)
-        return remote(wf.at[p], wf.at[p], nb_s.at[d, i], nb_r.at[d, i], peers[ndims[d]])
+        p = piece(far_f, covers[i][1], i)
+        return remote(wf.at[p], wf.at[p], nb_s.at[d, i], nb_r.at[d, i], peers[covers[i][0][d]])
 
     def pass_copy(j, i):
-        p = piece(far_f, colour if j == 0 else others[j - 1], i)
+        p = piece(far_f, covers[i][1] if j == 0 else covers[i][2][j - 1], i)
+        if i >= NEAR:
+            p = (whole(far_f), p[1])
         return remote(wf.at[p], wf.at[p], sf_s.at[j, i], sf_r.at[j, i], sib)
 
     own_out = remote(w_hbm, wf.at[whole(f)], sib_s.at[0], sib_r.at[0], sib)
@@ -168,13 +183,8 @@
         far_copy(i).start()
     own_out.start()
 
-    def tot_copy(o):
-        p = peer(o)
-        return remote(tot.at[p], tin.at[s], tsem.at[0], tsem.at[1], (p, f))
-
-    @pl.loop(1, 32)
-    def _(o):
-        tot_copy(o).start()
+    for p in ring:
+        remote(tot.at[p], tin.at[s], tsem.at[0], tsem.at[1], (p, f)).start()
 
     tin[s] = tot[s]
     most = pl.ds(0, 31)
@@ -212,9 +222,8 @@
     def send(k, q):
         src, dst = ((up1, in1), (down1, ent), (up2, in2), (down2, adj))[k]
 
-        @pl.loop(1, 32)
-        def _(o):
-            transfer(k, q, peer(o)).start()
+        for p in ring:
+            transfer(k, q, p).start()
 
         if k % 2:
             dst[q, :, s] = src[q, s]
@@ -380,28 +389,28 @@
     dbt[...] = jnp.zeros_like(dbt)
     def from_far(i):
         far_copy(i).wait_recv()
-        for d in range(3):
+        for d in range(3 if i < NEAR else 0):
             near_copy(d, i).start()
         pass_copy(0, i).start()
 
     def from_near(i):
         for d in range(3):
-            p = piece(far_f, others[d], i)
-            remote(
-                wf.at[p], wf.at[p], nb_s.at[d, i], nb_r.at[d, i], peers[ndims[d]]
-            ).wait_recv()
+            p = piece(far_f, covers[i][2][d], i)
+            to = peers[covers[i][0][d]]
+            remote(wf.at[p], wf.at[p], nb_s.at[d, i], nb_r.at[d, i], to).wait_recv()
             pass_copy(1 + d, i).start()
 
     def from_sibling(i):
-        for j in range(4):
-            p = piece(sibfar_f, colour if j == 0 else others[j - 1], i)
+        for j in range(4 if i < NEAR else 1):
+            p = piece(sibfar_f, covers[i][1] if j == 0 else covers[i][2][j - 1], i)
+            if i >= NEAR:
+                p = (whole(sibfar_f), p[1])
             remote(wf.at[p], wf.at[p], sf_s.at[j, i], sf_r.at[j, i], sib).wait_recv()
 
     some(8)
     from_far(0)
     some(8)
     from_far(1)
-    some(4)
     from_near(0)
     from_far(2)
     some(4)
@@ -414,27 +423,26 @@
     from_near(2)
     from_far(4)
     from_sibling(1)
+    from_far(5)
+    from_near(3)
     from_sibling(2)
-    from_near(3)
-    from_far(5)
     project(0)
+    from_far(6)
     from_near(4)
-    from_far(6)
-    from_sibling(3)
     states(0)
     from_near(5)
-    from_far(7)
-    from_far(8)
+    from_sibling(3)
     from_sibling(4)
     project(1)
     from_near(6)
     states(1)
-    from_near(7)
-    from_near(8)
+    some(4)
     from_sibling(5)
     from_sibling(6)
+    from_far(7)
     project(2)
     states(2)
+    from_far(8)
     from_sibling(7)
     from_sibling(8)
     project(3)
@@ -442,10 +450,9 @@
     some(H)
     local_forward(0)
     local_forward(1)
-    remote(
-        tin.at[most], tin.at[most], tsem.at[0], tsem.at[1], sib
-    ).wait_recv()
+    remote(tin.at[most], tin.at[most], tsem.at[0], tsem.at[1], sib).wait_recv()
     tin[...] = jnp.exp(tin[...])
+    scan(0, 0, 0, 1)
 
     def block(r):
         p = here
@@ -474,33 +481,72 @@
         dbt[...] += mm(xt[ctall, :], ga, NT)
         g[:, INNER + N : COLS] = dct[...].astype(BF).T
 
-    def product(c, half):
+    def product(u, half):
+        c, _, n, col = UNITS[u]
         ids = order(c)[32 * half : 32 * half + 32]
         la = jnp.concatenate([ta[r] for r in ids], axis=0)
         lb = jnp.concatenate([tb[r] for r in ids], axis=0)
-        cols = pl.ds(c * CW, CW)
+        cols = pl.ds(col, n)
         v = mm(la, g[:, cols], NN) + mm(lb, gs[:, cols], NN)
-        return v.reshape(32, 16, CW).astype(BF)
-
-    def halve(c, k):
-        p = pl.ds(OFF[k], 32 >> k)
-        return remote(sb.at[c, p], rb.at[c, p], wsem.at[c, k], wrsem.at[c, k], peers[(c + k) % 6])
-
-    def direct(c, i):
-        dims = [(c + 3 + b) % 6 for b in range(3) if (i >> (2 - b)) & 1]
+        return v.reshape(32, 16, n).astype(BF)
+
+    def lanes(u):
+        return pl.ds(UNITS[u][1], UNITS[u][2])
+
+    def halve(u, k):
+        c = UNITS[u][0]
+        p = (c, pl.ds(OFF[k], 32 >> k), slice(None), lanes(u))
+        return remote(sb.at[p], rb.at[p], wsem.at[u, k], wrsem.at[u, k], peers[(c + 5 + k) % 6])
+
+    def direct(u, i):
+        c = UNITS[u][0]
+        dims = [(c + 8 + b) % 6 for b in range(3) if (i >> (2 - b)) & 1]
         return remote(
-            part.at[c, i], rb.at[c, OFF[3] + i - 1], wsem.at[c, 3], wrsem.at[c, 3], across(dims)
+            part.at[c, i, :, lanes(u)], rb.at[c, OFF[3] + i - 1, :, lanes(u)],
+            wsem.at[u, 3], wrsem.at[u, 3], across(dims),
         )
 
-    def first(c):
-        sb[c, pl.ds(0, 32)] = product(c, 1)
-        halve(c, 0).start()
+    def first(*units):
+        for u in units:
+            sb[UNITS[u][0], pl.ds(0, 32), :, lanes(u)] = product(u, 1)
+            halve(u, 0).start()
+
+    def keep(*units):
+        for u in units:
+            part[UNITS[u][0], pl.ds(0, 32), :, lanes(u)] = product(u, 0)
+
+    def step(k, *units):
+        n = 64 >> k
+        m = n // 2
+        for u in units:
+            c, w = UNITS[u][0], lanes(u)
+            halve(u, k - 1).wait_recv()
+            if k < 3:
+                got = rb[c, pl.ds(OFF[k - 1] + m, m), :, w]
+                sb[c, pl.ds(OFF[k], m), :, w] = part[c, pl.ds(m, m), :, w] + got
+                halve(u, k).start()
+                part[c, pl.ds(0, m), :, w] += rb[c, pl.ds(OFF[k - 1], m), :, w]
+            else:
+                part[c, pl.ds(0, n), :, w] += rb[c, pl.ds(OFF[k - 1], n), :, w]
+        if k == 3:
+            for u in units:
+                for i in range(7, 0, -1):
+                    direct(u, i).start()
+
+    def last_step(*units):
+        for u in units:
+            c, w = UNITS[u][0], lanes(u)
+            p = rb.at[c, pl.ds(OFF[3], 7), :, w]
+            remote(p, p, wsem.at[u, 3], wrsem.at[u, 3], sib).wait_recv()
+            v = part[c, 0, :, w].astype(F32)
+            for i in range(7):
+                v = v + rb[c, OFF[3] + i, :, w].astype(F32)
+            gw_ref[:, pl.ds(UNITS[u][3], UNITS[u][2])] = v
 
     def tokens_part(i):
         r = pl.ds(512 * i, 512)
         tok[:, r] = mm(g[...], wf[r, :], NT).astype(BF)
 
-    scan(0, 0, 0, 1)
     scan(0, 1, 0, 1)
     local_forward(2)
     scan(0, 2, 0, 1)
@@ -515,69 +561,57 @@
     mixture(3)
     scan(2, 1, 1, 0)
     local_backward(2)
-    give_output()
+    relay_tokens()
+    finish(0)
     scan(2, 2, 1, 0)
     local_backward(3)
-    relay_tokens()
-    finish(0)
+    g_copy(0).wait_recv()
+    first(0, 1)
+    finish(1)
     scan(2, 3, 1, 0)
     close_affinity()
-    finish(1)
-    g_copy(0).wait_recv()
-    first(0)
+    keep(0, 1)
+    g_copy(1).wait_recv()
+    first(2, 3)
+    give_output()
+    keep(2, 3)
     finish(2)
-    g_copy(1).wait_recv()
-    first(1)
+    step(1, 0, 1)
+    g_copy(2).wait_recv()
+    first(4, 5)
     finish(3)
     g[:, INNER : INNER + N] = dbt[...].astype(BF).T
     g_copy(4).start()
-    g_copy(2).wait_recv()
-    first(2)
-    first(3)
     g_copy(3).wait_recv()
-    first(4)
+    first(6, 7, 8, 9)
     g_copy(4).wait_recv()
-    first(5)
-    for c in range(6):
-        part[c] = product(c, 0)
+    first(10, 11)
+    step(1, 2, 3)
+    keep(4, 5)
+    keep(6, 7, 8, 9, 10, 11)
+    step(2, 0, 1)
     tokens_part(0)
     tokens_part(1)
+    step(1, 4, 5)
+    step(1, 6, 7, 8, 9, 10, 11)
     tokens_part(2)
+    step(2, 2, 3)
+    step(3, 0, 1)
     tokens_part(3)
     gt_copy = pltpu.make_async_copy(tok, gt_hbm, lsem.at[4])
     gt_copy.start()
-    for k in range(1, 4):
-        n = 64 >> k
-        m = n // 2
-        for c in range(6):
-            halve(c, k - 1).wait_recv()
-            if k < 3:
-                sb[c, pl.ds(OFF[k], m)] = part[c, pl.ds(m, m)] + rb[c, pl.ds(OFF[k - 1] + m, m)]
-                halve(c, k).start()
-            else:
-                part[c, pl.ds(0, n)] += rb[c, pl.ds(OFF[k - 1], n)]
-                for i in range(7, 0, -1):
-                    if c > 0:
-                        direct(c - 1, i).start()
-        if k == 3:
-            for i in range(7, 0, -1):
-                direct(5, i).start()
-        if k < 3:
-            for c in range(6):
-                part[c, pl.ds(0, m)] += rb[c, pl.ds(OFF[k - 1], m)]
-    rest = pl.ds(OFF[3], 7)
-    for c in range(6):
-        remote(rb.at[c, rest], rb.at[c, rest], wsem.at[c, 3], wrsem.at[c, 3], sib).wait_recv()
-        v = part[c, 0].astype(F32)
-        for i in range(7):
-            v = v + rb[c, OFF[3] + i].astype(F32)
-        gw_ref[:, pl.ds(c * CW, CW)] = v
+    step(2, 4, 5)
+    step(2, 6, 7, 8, 9, 10, 11)
+    step(3, 2, 3)
+    step(3, 4, 5)
+    step(3, 6, 7, 8, 9, 10, 11)
+    last_step(0, 1, 2, 3, 4, 5, 6, 7, 8, 9, 10, 11)
 
     for i in range(PIECES):
         far_copy(i).wait_send()
-        for d in range(3):
+        for d in range(3 if i < NEAR else 0):
             near_copy(d, i).wait_send()
-        for j in range(4):
+        for j in range(4 if i < NEAR else 1):
             pass_copy(j, i).wait_send()
     own_out.wait_send()
     tok_out.wait_send()
@@ -587,36 +621,44 @@
             left(k, q)
     for q in range(5):
         g_copy(q).wait_send()
-    for c in range(6):
+    for u in range(12):
         for k in range(3):
-            halve(c, k).wait_send()
-        sent = pl.ds(1, 7)
-        remote(
-            part.at[c, sent], part.at[c, sent], wsem.at[c, 3], wrsem.at[c, 3], sib
-        ).wait_send()
+            halve(u, k).wait_send()
+        p = part.at[UNITS[u][0], pl.ds(1, 7), :, lanes(u)]
+        remote(p, p, wsem.at[u, 3], wrsem.at[u, 3], sib).wait_send()
     out_copy.wait()
     gt_copy.wait()
 
 
-def settle_kernel(a, b, c, a2, b2, c2):
-    a2[...] = a[...]
-    b2[...] = b[...]
-    c2[...] = c[...]
+def settle_kernel(a, b, c, a2, b2, c2, va, vb, vc, sem):
+    moves = [(a.at[0, pl.ds(64 * i, 64)], va.at[pl.ds(64 * i, 64)], a2.at[0, pl.ds(64 * i, 64)]) for i in range(4)]
+    moves += [(b.at[0, pl.ds(64 * i, 64)], vb.at[pl.ds(64 * i, 64)], b2.at[0, pl.ds(64 * i, 64)]) for i in range(4)]
+    moves.append((c, vc, c2))
+    ins = [pltpu.make_async_copy(m[0], m[1], sem.at[0, i]) for i, m in enumerate(moves)]
+    outs = [pltpu.make_async_copy(m[1], m[2], sem.at[1, i]) for i, m in enumerate(moves)]
+    for m in ins:
+        m.start()
+    for m, n in zip(ins, outs):
+        m.wait()
+        n.start()
+    for n in outs:
+        n.wait()
 
 
 def settle(*arrays):
-    specs = [
-        pl.BlockSpec((1, T // 2, INNER), lambda i: (0, i, 0)),
-        pl.BlockSpec((1, T // 2, D), lambda i: (0, i, 0)),
-        pl.BlockSpec((16, COLS // 2), lambda i: (0, i)),
-    ]
+    v = pl.BlockSpec(memory_space=pl.ANY)
     return pl.pallas_call(
         settle_kernel,
         name="settle",
-        grid=(2,),
         out_shape=tuple(jax.ShapeDtypeStruct(v.shape, v.dtype) for v in arrays),
-        in_specs=specs,
-        out_specs=tuple(specs),
+        in_specs=[v] * 3,
+        out_specs=(v,) * 3,
+        scratch_shapes=[
+            pltpu.VMEM((T, INNER), BF),
+            pltpu.VMEM((T, D), BF),
+            pltpu.VMEM((16, COLS), F32),
+            pltpu.SemaphoreType.DMA((2, 9)),
+        ],
         compiler_params=pltpu.CompilerParams(vmem_limit_bytes=60 * 1024 * 1024),
     )(*arrays)
 
@@ -685,8 +727,8 @@
             dma((4, 4)),
             dma((4, 4)),
             dma((2,)),
-            dma((6, 4)),
-            dma((6, 4)),
+            dma((12, 4)),
+            dma((12, 4)),
         ],
         compiler_params=pltpu.CompilerParams(
             collective_id=0, has_side_effects=True, vmem_limit_bytes=60 * 1024 * 1024

time: 117 us -> 112 us (0.957)
  Pallas kernels: 116 us -> 111 us
    pallas_call x1, Pallas kernels: 113 us -> 109 us  [on_device(): pl.pallas_call(kernel, name='mixer_step', out_shape=(jax.ShapeDtypeStruct...]
where the time goes in v5:
time: 112 us
  Pallas kernels  111 us (99%)
    pallas_call x1, Pallas kernels, on_device(): pl.pallas_call(kernel, name='mixer_step', out_shape=(jax.ShapeDtypeStruct...  109 us
    pallas_call x1, Pallas kernels, settle(): pl.pallas_call(settle_kernel, name='settle', out_shape=tuple((jax.ShapeDt...  2.46 us

profile of v5, /device:TPU:0, one launch (start us, length us, event | category | flops | bytes accessed | tf_op | source)
XLA Modules:
  0.0 112.0 jit_solution(10271947016061115265)
XLA Ops:
  0.6 108.7 %mixer_step.1 = (bf16[256,2048]{1,0:T(8,128)(2,1)}, bf16[256,2048]{1,0:T(8,128)(2,1)}, f32[16,2304]{1,0:T(8,128)}) custom-call(bf16[256,2048]{1,0:T(8,128)(2,1)} %bitcast.5, bf16[512,2304]{1,0:T(8,128)(2,1)} %w_hbm.1, f32[32,256]{1,0:T(8,128)} %bitcast.9, bf16[256,2048]{1,0:T(8,128)(2,1)} %bitcast.6), custom_call_target="tpu_custom_call" | custom-call | tf_op jit(solution)/shard_map/mixer_step/pallas_call | solution.py:673
  109.4 2.5 %settle.1 = (bf16[1,256,2048]{2,1,0:T(8,128)(2,1)}, bf16[1,256,2048]{2,1,0:T(8,128)(2,1)}, f32[16,2304]{1,0:T(8,128)}) custom-call(bf16[1,256,2048]{2,1,0:T(8,128)(2,1)} %bitcast.7, bf16[1,256,2048]{2,1,0:T(8,128)(2,1)} %bitcast.8, f32[16,2304]{1,0:T(8,128)} %get-tuple-element.8.c), custom_call_target="tpu_custom_call" | custom-call | tf_op jit(solution)/shard_map/settle/pallas_call | solution.py:650

commit v6 on v5

--- a/solution.py
+++ b/solution.py
@@ -91,7 +91,7 @@
     pys = [4 * lax.rem(y_ + d, 4) for d in range(4)]
     pzs = [16 * lax.rem(zl + d, 2) for d in range(2)]
     pyz = [a + b for a in pzs for b in pys]
-    ring = [pyz[o // 4] + pxs[o % 4] for o in range(1, 32)]
+    ring = [pzs[o // 16] + pys[o % 4] + pxs[(o // 4) % 4] for o in range(1, 32)]
 
     for p in ring:
         pl.semaphore_signal(barrier, inc=1, device_id=(p, f), device_id_type=MESH)
@@ -565,15 +565,17 @@
     finish(0)
     scan(2, 2, 1, 0)
     local_backward(3)
-    g_copy(0).wait_recv()
-    first(0, 1)
-    finish(1)
     scan(2, 3, 1, 0)
     close_affinity()
-    keep(0, 1)
+    g_copy(0).wait_recv()
+    first(0)
+    keep(0)
+    finish(1)
+    first(1)
+    keep(1)
+    give_output()
     g_copy(1).wait_recv()
     first(2, 3)
-    give_output()
     keep(2, 3)
     finish(2)
     step(1, 0, 1)

time: 112 us -> 111 us (level)
  no operation moved by 1% of the time
where the time goes in v6:
time: 111 us
  Pallas kernels  110 us (99%)
    pallas_call x1, Pallas kernels, on_device(): pl.pallas_call(kernel, name='mixer_step', out_shape=(jax.ShapeDtypeStruct...  108 us
    pallas_call x1, Pallas kernels, settle(): pl.pallas_call(settle_kernel, name='settle', out_shape=tuple((jax.ShapeDt...  2.46 us

profile of v6, /device:TPU:0, one launch (start us, length us, event | category | flops | bytes accessed | tf_op | source)
XLA Modules:
  0.0 110.9 jit_solution(14964600050443864932)
XLA Ops:
  0.6 107.6 %mixer_step.1 = (bf16[256,2048]{1,0:T(8,128)(2,1)}, bf16[256,2048]{1,0:T(8,128)(2,1)}, f32[16,2304]{1,0:T(8,128)}) custom-call(bf16[256,2048]{1,0:T(8,128)(2,1)} %bitcast.5, bf16[512,2304]{1,0:T(8,128)(2,1)} %w_hbm.1, f32[32,256]{1,0:T(8,128)} %bitcast.9, bf16[256,2048]{1,0:T(8,128)(2,1)} %bitcast.6), custom_call_target="tpu_custom_call" | custom-call | tf_op jit(solution)/shard_map/mixer_step/pallas_call | solution.py:675
  108.2 2.5 %settle.1 = (bf16[1,256,2048]{2,1,0:T(8,128)(2,1)}, bf16[1,256,2048]{2,1,0:T(8,128)(2,1)}, f32[16,2304]{1,0:T(8,128)}) custom-call(bf16[1,256,2048]{2,1,0:T(8,128)(2,1)} %bitcast.7, bf16[1,256,2048]{2,1,0:T(8,128)(2,1)} %bitcast.8, f32[16,2304]{1,0:T(8,128)} %get-tuple-element.8.c), custom_call_target="tpu_custom_call" | custom-call | tf_op jit(solution)/shard_map/settle/pallas_call | solution.py:652
